TPU v7x, 32 devices: a whole 2x2x4 slice. The times are simulated.
32 devices in a mesh: gx: 8 (over z, y), gy: 4 (over x, core).
Axes of the slice: x: 2, y: 2, z: 4, core: 2. Of those that a mesh axis runs over, the one named last changes fastest.
Arguments:
- cotangent: float32 [2, 128, 1536], P(None, 'gx', 'gy'), may hold values from -12 to 12
- velocity_in: bfloat16 [2, 128, 1536], P(None, 'gx', 'gy'), may hold values from -6 to 6
- hidden_pre1: bfloat16 [64, 128, 1536], P(None, 'gx', 'gy'), may hold values from -6 to 6
- hidden_pre2: bfloat16 [64, 128, 1536], P(None, 'gx', 'gy'), may hold values from -6 to 6
- w_first: bfloat16 [9, 64, 2], replicated, may hold values from -1.5 to 1.5
- w_middle: bfloat16 [9, 64, 64], replicated, may hold values from -0.25 to 0.25
- w_last: bfloat16 [9, 2, 64], replicated, may hold values from -0.25 to 0.25
Outputs:
- grad_velocity: float32 [2, 128, 1536], P(None, 'gx', 'gy')
- grad_first: float32 [9, 64, 2], replicated
- grad_middle: float32 [9, 64, 64], replicated
- grad_last: float32 [9, 2, 64], replicated
- grad_bias1: float32 [64], replicated
- grad_bias2: float32 [64], replicated
All inputs are finite; a program needn't handle non-finite values.
Results may differ from a plain program's by a relative error of at most 0.0075.
Values may be sent and summed in bfloat16 or wider, within the bound.
A program may use at most 64 MiB of HBM per device.

v0:
```python
import math

import jax
import jax.numpy as jnp
from jax import lax
from jax.sharding import PartitionSpec as P

ITERS = 4


OFFSETS = ((-1, -1), (-1, 0), (-1, 1), (0, -1), (0, 0), (0, 1), (1, -1), (1, 0), (1, 1))


def with_halo(shard, sides, width):
    for axis, dim in sides:
        count, length = (lax.axis_size(axis), shard.shape[dim])
        up = [(i, (i + 1) % count) for i in range(count)]
        down = [(j, i) for i, j in up]
        last = lax.slice_in_dim(shard, length - width, length, axis=dim)
        leading = lax.slice_in_dim(shard, 0, width, axis=dim)
        before = lax.ppermute(last, axis, up)
        after = lax.ppermute(leading, axis, down)
        shard = jnp.concatenate([before, shard, after], axis=dim)
    return shard


def gelu_slope(pre):
    values = pre.astype(jnp.float32)
    _, pullback = jax.vjp(lambda inner: jax.nn.gelu(inner, approximate=True), values)
    return pullback(jnp.ones_like(values))[0]


def window(padded, row_step, col_step, rows, cols):
    return padded[:, 1 + row_step : 1 + row_step + rows, 1 + col_step : 1 + col_step + cols]


def channel_border(field):
    return with_halo(field, (("gx", 1), ("gy", 2)), 1)


def stencil_apply(field):
    padded = with_halo(field, (("gx", 0), ("gy", 1)), 2)
    beside = padded[:-4, 2:-2] + padded[4:, 2:-2] + padded[2:-2, :-4]
    beside = beside + padded[2:-2, 4:]
    return (padded, field - 0.25 * beside)


def paired_sums(residual, image):
    return lax.psum((jnp.sum(residual * residual), jnp.sum(residual * image)), ("gx", "gy"))


def conv_back(weights, padded, rows, cols):
    channels = padded.shape[0]
    total = jnp.zeros((weights.shape[2], rows * cols), jnp.float32)
    for index, (row_step, col_step) in enumerate(OFFSETS):
        shifted = window(padded, -row_step, -col_step, rows, cols).reshape(channels, -1)
        total = total + lax.dot_general(
            weights[index], shifted, (((0,), (0,)), ((), ())), preferred_element_type=jnp.float32
        )
    return total.reshape(weights.shape[2], rows, cols)


def grads_from_padded_deltas(delta_pad, inputs, rows, cols):
    flat_inputs = inputs.reshape(inputs.shape[0], -1)
    results = []
    for row_step, col_step in OFFSETS:
        shifted = window(delta_pad, -row_step, -col_step, rows, cols).reshape(
            delta_pad.shape[0], -1
        )
        results.append(
            lax.dot_general(
                shifted, flat_inputs, (((1,), (1,)), ((), ())), preferred_element_type=jnp.float32
            )
        )
    return jnp.stack(results)


def per_device(cotangent, velocity_in, hidden_pre1, hidden_pre2, w_first, w_middle, w_last):
    rows = cotangent.shape[1]
    cols = cotangent.shape[2]
    factor = 1.0 / math.sqrt(rows * lax.axis_size("gx") * cols * lax.axis_size("gy"))
    hidden1 = jax.nn.gelu(hidden_pre1.astype(jnp.float32), approximate=True).astype(jnp.bfloat16)
    hidden2 = jax.nn.gelu(hidden_pre2.astype(jnp.float32), approximate=True).astype(jnp.bfloat16)
    slope1 = gelu_slope(hidden_pre1)
    slope2 = gelu_slope(hidden_pre2)
    cot_pad = with_halo(cotangent, (("gx", 1), ("gy", 2)), 1)
    along_rows = cot_pad[0, 2:, 1:-1] - cot_pad[0, :-2, 1:-1]
    along_cols = cot_pad[1, 1:-1, 2:] - cot_pad[1, 1:-1, :-2]
    rhs = -0.5 * (along_rows + along_cols)
    lam_pad = jnp.zeros((rows + 4, cols + 4), jnp.float32)
    residual = rhs
    resid_pad, image = stencil_apply(residual)
    norm_now, product = paired_sums(residual, image)
    alpha = norm_now / product
    dir_pad = resid_pad
    along = image
    for step in range(ITERS):
        lam_pad = lam_pad + alpha * dir_pad
        if step + 1 < ITERS:
            residual = residual - alpha * along
            resid_pad, image = stencil_apply(residual)
            norm_next, product = paired_sums(residual, image)
            ratio = norm_next / norm_now
            alpha = norm_next / (product - ratio * norm_next / alpha)
            dir_pad = resid_pad + ratio * dir_pad
            along = image + ratio * along
            norm_now = norm_next
    adjoint_rows = 0.5 * (lam_pad[0 : rows + 2, 1 : cols + 3] - lam_pad[2 : rows + 4, 1 : cols + 3])
    adjoint_cols = 0.5 * (lam_pad[1 : rows + 3, 0 : cols + 2] - lam_pad[1 : rows + 3, 2 : cols + 4])
    adjoint_pad = cot_pad + jnp.stack([adjoint_rows, adjoint_cols])
    adjoint_b = adjoint_pad.astype(jnp.bfloat16)
    delta2 = (conv_back(w_last, adjoint_b, rows, cols) * slope2).astype(jnp.bfloat16)
    delta2_pad = channel_border(delta2)
    delta1 = (conv_back(w_middle, delta2_pad, rows, cols) * slope1).astype(jnp.bfloat16)
    grad_last = grads_from_padded_deltas(adjoint_b, hidden2, rows, cols)
    grad_middle = grads_from_padded_deltas(delta2_pad, hidden1, rows, cols)
    delta1_pad = channel_border(delta1)
    spread = conv_back(w_first, delta1_pad, rows, cols)
    grad_first = grads_from_padded_deltas(delta1_pad, velocity_in, rows, cols)
    grad_velocity = adjoint_pad[:, 1:-1, 1:-1] + spread
    bias_one = jnp.sum(delta1.astype(jnp.float32), axis=(1, 2))
    bias_two = jnp.sum(delta2.astype(jnp.float32), axis=(1, 2))
    summed = lax.psum((grad_first, grad_middle, grad_last, bias_one, bias_two), ("gx", "gy"))
    return (
        grad_velocity,
        factor * summed[0],
        factor * summed[1],
        factor * summed[2],
        factor * summed[3],
        factor * summed[4],
    )


def solution(mesh):
    return jax.shard_map(
        per_device,
        mesh=mesh,
        in_specs=(
            P(None, "gx", "gy"),
            P(None, "gx", "gy"),
            P(None, "gx", "gy"),
            P(None, "gx", "gy"),
            P(),
            P(),
            P(),
        ),
        out_specs=(P(None, "gx", "gy"), P(), P(), P(), P(), P()),
        check_vma=False,
    )
```

profile of v0, /device:TPU:0, one launch (start us, length us, event | category | flops | bytes accessed | tf_op | source)
XLA Modules:
  0.0 422.6 jit_solution(12630795308313707400)
XLA Ops:
  8.0 3.0 collective-permute-start
  11.0 3.1 collective-permute-start.1
  14.1 1.5 collective-permute-done
  16.9 1.1 collective-permute-done.3
  18.0 1.8 collective-permute-done.2
  20.8 1.6 collective-permute-start.4
  22.4 3.4 collective-permute-start.5
  25.7 1.5 collective-permute-done.4
  27.3 1.7 collective-permute-start.7
  29.1 1.4 collective-permute-done.6
  31.2 40.4 %all-reduce.4 = (f32[]{:T(128)}, f32[]{:T(128)}) all-reduce(f32[]{:T(128)} %get-tuple-element.25, f32[]{:T(128)} %get-tuple-element.24), channel_id=1, replica_groups=mesh['gx'=8,'gy'=4] {'gx','gy'}, use_global_device_ids=true, to_apply=%region_1.0 | all-reduce | flops 2 | bytes 16 | tf_op jit(solution)/shard_map/psum | solution.py:49
  72.9 2.5 collective-permute-start.8
  75.5 2.3 collective-permute-start.9
  77.7 1.6 collective-permute-done.8
  79.4 1.7 collective-permute-start.11
  81.1 1.4 collective-permute-done.10
  83.2 41.5 %all-reduce.3 = (f32[]{:T(128)}, f32[]{:T(128)}) all-reduce(f32[]{:T(128)} %get-tuple-element.23, f32[]{:T(128)} %get-tuple-element.22), channel_id=1, replica_groups=mesh['gx'=8,'gy'=4] {'gx','gy'}, use_global_device_ids=true, to_apply=%region_5.0 | all-reduce | flops 2 | bytes 16 | tf_op jit(solution)/shard_map/psum | solution.py:49
  129.4 2.5 collective-permute-start.12
  131.9 2.3 collective-permute-start.13
  134.2 1.6 collective-permute-done.12
  135.8 1.7 collective-permute-start.15
  137.6 1.4 collective-permute-done.14
  139.7 41.2 %all-reduce.2 = (f32[]{:T(128)}, f32[]{:T(128)}) all-reduce(f32[]{:T(128)} %get-tuple-element.21, f32[]{:T(128)} %get-tuple-element.20), channel_id=1, replica_groups=mesh['gx'=8,'gy'=4] {'gx','gy'}, use_global_device_ids=true, to_apply=%region_9.0 | all-reduce | flops 2 | bytes 16 | tf_op jit(solution)/shard_map/psum | solution.py:49
  185.0 2.5 collective-permute-start.16
  187.5 2.3 collective-permute-start.17
  189.8 1.6 collective-permute-done.16
  191.4 1.7 collective-permute-start.19
  195.3 41.5 %all-reduce.1 = (f32[]{:T(128)}, f32[]{:T(128)}) all-reduce(f32[]{:T(128)} %get-tuple-element.19, f32[]{:T(128)} %get-tuple-element.18), channel_id=1, replica_groups=mesh['gx'=8,'gy'=4] {'gx','gy'}, use_global_device_ids=true, to_apply=%region_13.0 | all-reduce | flops 2 | bytes 16 | tf_op jit(solution)/shard_map/psum | solution.py:49
  245.9 1.4 convert_reduce_fusion
  250.4 2.5 collective-permute-start.20
  252.9 2.3 collective-permute-start.21
  255.6 1.7 collective-permute-done.20
  257.7 1.7 collective-permute-start.22
  259.8 4.9 %collective-permute-done.23 = bf16[64,18,1]{2,0,1:T(8,128)(2,1)S(1)} collective-permute-done((bf16[64,18,1]{2,0,1:T(8,128)(2,1)S(1)}, bf16[64,18,1]{2,0,1:T(8,128)(2,1)S(1)}, u32[]{:S(2)}, u32[]{:S(2)}) %collective-permute-start.23) | collective-permute-done | bytes 2336 | tf_op jit(solution)/shard_map/ppermute | solution.py:21
  264.7 1.8 collective-permute-done.22
  268.3 1.2 slice_bitcast_fusion.6
  279.8 1.2 convert_reduce_fusion.1
  281.1 1.8 collective-permute-start.24
  282.9 3.2 collective-permute-start.25
  289.8 1.9 collective-permute-start.26
  291.9 1.0 copy.83
  293.9 2.9 collective-permute-done.27
  296.8 2.7 collective-permute-done.26
  301.5 1.6 slice_bitcast_fusion
  305.8 39.8 %all-reduce = (f32[9,64,2]{1,2,0:T(2,128)S(1)}, f32[9,2,64]{2,1,0:T(2,128)S(1)}, f32[64]{0:T(128)S(1)}, f32[64]{0:T(128)S(1)}) all-reduce(f32[9,64,2]{1,2,0:T(2,128)S(1)} %fusion.40, f32[9,2,64]{2,1,0:T(2,128)S(1)} %fusion.31, f32[64]{0:T(128)S(1)} %get-tuple-element.40, ...), channel_id=1, replica_groups=mesh['gx'=8,'gy'=4] {'gx','gy'}, use_global_device_ids=true, to_apply=%region_16.0 | all-reduce | flops 2432 | bytes 19456 | tf_op jit(solution)/shard_map/psum | solution.py:123
  347.4 1.3 copy.84
  353.5 60.6 %all-reduce.7.cloned.1.call-done = f32[9,64,64]{2,1,0:T(8,128)} async-done(((f32[9,64,64]{2,1,0:T(8,128)}), f32[9,64,64]{2,1,0:T(8,128)}) %all-reduce.7.cloned.1.call-update) | async-done | bytes 147472 | tf_op jit(solution)/shard_map/psum | solution.py:123
  414.1 1.7 broadcast_multiply_fusion
  (157 shorter events, 45.2 us)
Async XLA Ops:
  7.2 293.9 %copy-start = (bf16[2,16,384]{2,1,0:T(8,128)(2,1)S(1)}, bf16[2,16,384]{2,1,0:T(8,128)(2,1)}, u32[]{:S(2)}) copy-start(bf16[2,16,384]{2,1,0:T(8,128)(2,1)} %param.8) | copy-start | bytes 73732
  7.2 234.3 %copy-start.11 = (bf16[9,2,64]{2,1,0:T(2,128)(2,1)S(1)}, bf16[9,2,64]{2,1,0:T(2,128)(2,1)}, u32[]{:S(2)}) copy-start(bf16[9,2,64]{2,1,0:T(2,128)(2,1)} %param.13) | copy-start | bytes 6916
  7.2 406.9 %all-reduce.7.cloned.1.call-start = ((), (), s32[]{:S(2)}) async-start(), calls=%async_computation | async-start | bytes 589824 | tf_op jit(solution)/shard_map/psum | solution.py:123
  8.0 7.6 %collective-permute-start = (f32[2,1,384]{2,1,0:T(1,128)S(1)}, f32[2,1,384]{2,1,0:T(1,128)S(1)}, u32[]{:S(2)}, u32[]{:S(2)}) collective-permute-start(f32[2,1,384]{2,1,0:T(1,128)S(1)} %get-tuple-element.78), channel_id=1, source_target_pairs={{0,4},{4,8},{8,12},{12,16},{16,20},{20,24},{24,28},{28,0},{1,5},{5... | collective-permute-start | bytes 9224 | tf_op jit(solution)/shard_map/ppermute | solution.py:21
  11.0 4.6 %collective-permute-start.1 = (f32[2,1,384]{2,1,0:T(1,128)S(1)}, f32[2,1,384]{2,1,0:T(1,128)S(1)}, u32[]{:S(2)}, u32[]{:S(2)}) collective-permute-start(f32[2,1,384]{2,1,0:T(1,128)S(1)} %get-tuple-element.79), channel_id=1, source_target_pairs={{4,0},{8,4},{12,8},{16,12},{20,16},{24,20},{28,24},{0,28},{5,1},{9... | collective-permute-start | bytes 9224 | tf_op jit(solution)/shard_map/ppermute | solution.py:22
  16.4 1.6 collective-permute-start.3
  16.5 3.4 collective-permute-start.2
  20.8 6.5 %collective-permute-start.4 = (f32[2,384]{1,0:T(2,128)S(1)}, f32[2,384]{1,0:T(2,128)S(1)}, u32[]{:S(2)}, u32[]{:S(2)}) collective-permute-start(f32[2,384]{1,0:T(2,128)S(1)} %get-tuple-element.103), channel_id=1, source_target_pairs={{0,4},{4,8},{8,12},{12,16},{16,20},{20,24},{24,28},{28,0},{1,5},{5... | collective-permute-start | bytes 9224 | tf_op jit(solution)/shard_map/ppermute | solution.py:21
  22.4 4.9 %collective-permute-start.5 = (f32[2,384]{1,0:T(2,128)S(1)}, f32[2,384]{1,0:T(2,128)S(1)}, u32[]{:S(2)}, u32[]{:S(2)}) collective-permute-start(f32[2,384]{1,0:T(2,128)S(1)} %get-tuple-element.104), channel_id=1, source_target_pairs={{4,0},{8,4},{12,8},{16,12},{20,16},{24,20},{28,24},{0,28},{5,1},{9... | collective-permute-start | bytes 9224 | tf_op jit(solution)/shard_map/ppermute | solution.py:22
  27.3 3.1 collective-permute-start.6
  27.3 3.1 collective-permute-start.7
  72.9 6.3 %collective-permute-start.8 = (f32[2,384]{1,0:T(2,128)S(1)}, f32[2,384]{1,0:T(2,128)S(1)}, u32[]{:S(2)}, u32[]{:S(2)}) collective-permute-start(f32[2,384]{1,0:T(2,128)S(1)} %get-tuple-element.101), channel_id=1, source_target_pairs={{0,4},{4,8},{8,12},{12,16},{16,20},{20,24},{24,28},{28,0},{1,5},{5... | collective-permute-start | bytes 9224 | tf_op jit(solution)/shard_map/ppermute | solution.py:21
  75.5 3.8 collective-permute-start.9
  79.4 3.1 collective-permute-start.10
  79.4 3.1 collective-permute-start.11
  129.4 6.3 %collective-permute-start.12 = (f32[2,384]{1,0:T(2,128)S(1)}, f32[2,384]{1,0:T(2,128)S(1)}, u32[]{:S(2)}, u32[]{:S(2)}) collective-permute-start(f32[2,384]{1,0:T(2,128)S(1)} %get-tuple-element.99), channel_id=1, source_target_pairs={{0,4},{4,8},{8,12},{12,16},{16,20},{20,24},{24,28},{28,0},{1,5},{5... | collective-permute-start | bytes 9224 | tf_op jit(solution)/shard_map/ppermute | solution.py:21
  131.9 3.8 collective-permute-start.13
  135.8 3.1 collective-permute-start.14
  135.8 3.1 collective-permute-start.15
  185.0 6.3 %collective-permute-start.16 = (f32[2,384]{1,0:T(2,128)S(1)}, f32[2,384]{1,0:T(2,128)S(1)}, u32[]{:S(2)}, u32[]{:S(2)}) collective-permute-start(f32[2,384]{1,0:T(2,128)S(1)} %get-tuple-element.97), channel_id=1, source_target_pairs={{0,4},{4,8},{8,12},{12,16},{16,20},{20,24},{24,28},{28,0},{1,5},{5... | collective-permute-start | bytes 9224 | tf_op jit(solution)/shard_map/ppermute | solution.py:21
  187.5 3.8 collective-permute-start.17
  191.4 3.1 collective-permute-start.18
  191.4 3.1 collective-permute-start.19
  244.8 1.1 copy-start.6
  250.4 6.9 %collective-permute-start.20 = (bf16[64,1,384]{2,0,1:T(8,128)(2,1)S(1)}, bf16[64,1,384]{2,0,1:T(8,128)(2,1)S(1)}, u32[]{:S(2)}, u32[]{:S(2)}) collective-permute-start(bf16[64,1,384]{2,0,1:T(8,128)(2,1)S(1)} %get-tuple-element.72), channel_id=1, source_target_pairs={{0,4},{4,8},{8,12},{12,16},{16,20},{20,24},{24,28},{28,0},{1,5},{5... | collective-permute-start | bytes 147464 | tf_op jit(solution)/shard_map/ppermute | solution.py:21
  252.9 4.6 %collective-permute-start.21 = (bf16[64,1,384]{2,0,1:T(8,128)(2,1)S(1)}, bf16[64,1,384]{2,0,1:T(8,128)(2,1)S(1)}, u32[]{:S(2)}, u32[]{:S(2)}) collective-permute-start(bf16[64,1,384]{2,0,1:T(8,128)(2,1)S(1)} %get-tuple-element.73), channel_id=1, source_target_pairs={{4,0},{8,4},{12,8},{16,12},{20,16},{24,20},{28,24},{0,28},{5,1},{9... | collective-permute-start | bytes 147464 | tf_op jit(solution)/shard_map/ppermute | solution.py:22
  257.7 7.0 %collective-permute-start.23 = (bf16[64,18,1]{2,0,1:T(8,128)(2,1)S(1)}, bf16[64,18,1]{2,0,1:T(8,128)(2,1)S(1)}, u32[]{:S(2)}, u32[]{:S(2)}) collective-permute-start(bf16[64,18,1]{2,0,1:T(8,128)(2,1)S(1)} %get-tuple-element.63), channel_id=1, source_target_pairs={{0,1},{1,2},{2,3},{3,0},{4,5},{5,6},{6,7},{7,4},{8,9},{9,10},{10,1... | collective-permute-start | bytes 6920 | tf_op jit(solution)/shard_map/ppermute | solution.py:21
  257.7 8.8 %collective-permute-start.22 = (bf16[64,18,1]{2,0,1:T(8,128)(2,1)S(1)}, bf16[64,18,1]{2,0,1:T(8,128)(2,1)S(1)}, u32[]{:S(2)}, u32[]{:S(2)}) collective-permute-start(bf16[64,18,1]{2,0,1:T(8,128)(2,1)S(1)} %get-tuple-element.64), channel_id=1, source_target_pairs={{1,0},{2,1},{3,2},{0,3},{5,4},{6,5},{7,6},{4,7},{9,8},{10,9},{11,1... | collective-permute-start | bytes 6920 | tf_op jit(solution)/shard_map/ppermute | solution.py:22
  259.8 7.5 %copy-start.7 = (bf16[64,16,384]{2,1,0:T(8,128)(2,1)S(1)}, bf16[64,16,384]{2,1,0:T(8,128)(2,1)}, u32[]{:S(2)}) copy-start(bf16[64,16,384]{2,1,0:T(8,128)(2,1)} %param.9) | copy-start | bytes 2359300
  275.1 0.9 copy-start.9
  281.1 8.5 %collective-permute-start.24 = (bf16[64,1,384]{2,0,1:T(8,128)(2,1)S(1)}, bf16[64,1,384]{2,0,1:T(8,128)(2,1)S(1)}, u32[]{:S(2)}, u32[]{:S(2)}) collective-permute-start(bf16[64,1,384]{2,0,1:T(8,128)(2,1)S(1)} %get-tuple-element.68), channel_id=1, source_target_pairs={{0,4},{4,8},{8,12},{12,16},{16,20},{20,24},{24,28},{28,0},{1,5},{5... | collective-permute-start | bytes 147464 | tf_op jit(solution)/shard_map/ppermute | solution.py:21
  282.9 6.7 %collective-permute-start.25 = (bf16[64,1,384]{2,0,1:T(8,128)(2,1)S(1)}, bf16[64,1,384]{2,0,1:T(8,128)(2,1)S(1)}, u32[]{:S(2)}, u32[]{:S(2)}) collective-permute-start(bf16[64,1,384]{2,0,1:T(8,128)(2,1)S(1)} %get-tuple-element.69), channel_id=1, source_target_pairs={{4,0},{8,4},{12,8},{16,12},{20,16},{24,20},{28,24},{0,28},{5,1},{9... | collective-permute-start | bytes 147464 | tf_op jit(solution)/shard_map/ppermute | solution.py:22
  287.8 0.7 copy-start.8
  289.7 7.1 %collective-permute-start.27 = (bf16[64,18,1]{2,0,1:T(8,128)(2,1)S(1)}, bf16[64,18,1]{2,0,1:T(8,128)(2,1)S(1)}, u32[]{:S(2)}, u32[]{:S(2)}) collective-permute-start(bf16[64,18,1]{2,0,1:T(8,128)(2,1)S(1)} %get-tuple-element.59), channel_id=1, source_target_pairs={{0,1},{1,2},{2,3},{3,0},{4,5},{5,6},{6,7},{7,4},{8,9},{9,10},{10,1... | collective-permute-start | bytes 6920 | tf_op jit(solution)/shard_map/ppermute | solution.py:21
  289.8 9.7 %collective-permute-start.26 = (bf16[64,18,1]{2,0,1:T(8,128)(2,1)S(1)}, bf16[64,18,1]{2,0,1:T(8,128)(2,1)S(1)}, u32[]{:S(2)}, u32[]{:S(2)}) collective-permute-start(bf16[64,18,1]{2,0,1:T(8,128)(2,1)S(1)} %get-tuple-element.60), channel_id=1, source_target_pairs={{1,0},{2,1},{3,2},{0,3},{5,4},{6,5},{7,6},{4,7},{9,8},{10,9},{11,1... | collective-permute-start | bytes 6920 | tf_op jit(solution)/shard_map/ppermute | solution.py:22
  305.5 43.2 %copy-start.2 = (bf16[16,8,8,384]{3,2,1,0:T(8,128)(2,1)S(1)}, bf16[16,8,8,384]{3,2,1,0:T(8,128)(2,1)}, u32[]{:S(2)}) copy-start(bf16[16,8,8,384]{3,2,1,0:T(8,128)(2,1)} %get-tuple-element.46) | copy-start | bytes 2359300
  347.4 1.4 copy-start.1
  349.0 0.7 copy-start.10
  349.1 1.1 copy-start.5
  349.7 1.2 copy-start.3
  350.6 1.2 copy-start.4
Sparse Core Ops, SparseCore 0:
  288.7 125.3 all-reduce.6
where the time goes:
time: 424 us; the launch traced here: 423 us
  blocking collectives  204 us (48%)
  waiting for transfers between devices  90.2 us (21%)
  starting transfers between devices  46.5 us (11%)
  between operations  28.6 us (7%)
  matrix products  23.8 us (6%)
  other arithmetic  15.2 us (4%)
  local copies, waits for them, and re-layouts  14.1 us (3%)
    psum x4, blocking collectives, paired_sums(): lax.psum((jnp.sum(residual * residual), jnp.sum(residual * image)), ('gx'...  164 us
    psum x1, waiting for transfers between devices, per_device(): lax.psum((grad_first, grad_middle, grad_last, bias_one, bias_two), ('gx',...  60.6 us
    psum x1, blocking collectives, per_device(): lax.psum((grad_first, grad_middle, grad_last, bias_one, bias_two), ('gx',...  39.8 us
    ppermute x14, starting transfers between devices, with_halo(): after = lax.ppermute(leading, axis, down)  29.5 us
    ppermute x14, waiting for transfers between devices, with_halo(): before = lax.ppermute(last, axis, up)  23.7 us
    ppermute x14, starting transfers between devices, with_halo(): before = lax.ppermute(last, axis, up)  17 us
    dot_general x27, matrix products, grads_from_padded_deltas(): lax.dot_general(shifted, flat_inputs, (((1,), (1,)), ((), ())), preferred...  14.4 us
    dot_general x27, matrix products, conv_back(): lax.dot_general(weights[index], shifted, (((0,), (0,)), ((), ())), prefer...  9.38 us
  transfers between devices with their start and end apart: 29, of which 18 were waited for; matrix products, arithmetic and copies ran while one was open for 5% of the time, Pallas kernels for 0%

commit v1 on v0

v1 whole, which is shorter than its diff:
```python
import functools
import math

import jax
import jax.numpy as jnp
from jax import lax
from jax.experimental import pallas as pl
from jax.experimental.pallas import tpu as pltpu
from jax.sharding import PartitionSpec as P

ITERS = 4
MESH = pl.DeviceIdType.MESH
NEIGHBOURS = tuple((dx, dy) for dx in (-1, 0, 1) for dy in (-1, 0, 1) if (dx, dy) != (0, 0))
NT = (((1,), (1,)), ((), ()))
NN = (((1,), (0,)), ((), ()))
C0 = 0.7978845608028654
C1 = 0.044715


def dot(a, b, dims):
    return lax.dot_general(a, b, dims, preferred_element_type=jnp.float32)


def roll_to(x, shift, axis):
    return pltpu.roll(x, shift % x.shape[axis], axis)


def gelu_value(v):
    return 0.5 * v * (1.0 + jnp.tanh(C0 * (v + C1 * (v * v * v))))


def gelu_slope(v):
    square = v * v
    t = jnp.tanh(C0 * (v + C1 * (square * v)))
    return 0.5 * (1.0 + t) + 0.5 * v * (1.0 - t * t) * (C0 * (1.0 + 3.0 * C1 * square))


def greet(peers):
    barrier = pltpu.get_barrier_semaphore()
    for peer in peers:
        pl.semaphore_signal(barrier, inc=1, device_id=peer, device_id_type=MESH)
    pl.semaphore_wait(barrier, len(peers))


def line_peers(nx, ny):
    gx, gy = lax.axis_index("gx"), lax.axis_index("gy")
    along_x = [(lax.rem(gx + k, nx), gy) for k in range(1, nx)]
    along_y = [(gx, lax.rem(gy + k, ny)) for k in range(1, ny)]
    return gx, gy, along_x, along_y


def merge_border(block, axis):
    n = block.shape[axis] - 256
    right = lax.slice_in_dim(block, n, n + 128, axis=axis)
    left = lax.slice_in_dim(block, n + 128, n + 256, axis=axis)
    lane = lax.broadcasted_iota(jnp.int32, right.shape, axis)
    border = jnp.where(lane < 64, right, left)
    return jnp.concatenate([lax.slice_in_dim(block, 0, n, axis=axis), border], axis=axis)


def exchange_kernel(
    nx, ny, cot, vel, pre1, pre2, adj_out, vel_out, pad1, pad2,
    cot_pad, slots_y, slots_x, send, recv, local, send_y, recv_y, send_x, recv_x,
):
    rows, cols = cot.shape[1], cot.shape[2]
    gx, gy, along_x, along_y = line_peers(nx, ny)

    def at(dx, dy):
        return (lax.rem(gx + dx + nx, nx), lax.rem(gy + dy + ny, ny))

    corners = [at(dx, dy) for dx, dy in NEIGHBOURS if dx and dy]
    greet(along_x + along_y + corners)

    def halves(dx, dy, halo):
        source = {1: slice(rows - halo, rows), 0: slice(0, rows), -1: slice(0, halo)}[dx]
        target = {1: slice(0, halo), 0: slice(halo, halo + rows), -1: slice(halo + rows, rows + 2 * halo)}[dx]
        lanes = {1: slice(cols - 128, cols), 0: slice(0, cols), -1: slice(0, 128)}[dy]
        land = {1: slice(cols + 128, cols + 256), 0: slice(0, cols), -1: slice(cols, cols + 128)}[dy]
        return source, target, lanes, land

    def border(index, which, dx, dy):
        if which < 2:
            src, dst = ((cot, cot_pad), (vel, vel_out))[which]
            s, t, a, b = halves(dx, dy, rows)
            src, dst = src.at[:, s, a], dst.at[:, t, b]
        else:
            src, dst = ((pre1, pad1), (pre2, pad2))[which - 2]
            s, t, a, b = halves(dx, dy, which - 1)
            src, dst = src.at[s, :, a], dst.at[t, :, b]
        return pltpu.make_async_remote_copy(
            src_ref=src, dst_ref=dst, send_sem=send.at[which, index], recv_sem=recv.at[which, index],
            device_id=at(dx, dy), device_id_type=MESH,
        )

    copies = [[border(i, which, dx, dy) for i, (dx, dy) in enumerate(NEIGHBOURS)] for which in range(4)]
    own = [
        pltpu.make_async_copy(pre1, pad1.at[1 : rows + 1, :, 0:cols], local.at[0]),
        pltpu.make_async_copy(pre2, pad2.at[2 : rows + 2, :, 0:cols], local.at[1]),
    ]
    for copy in copies[0]:
        copy.start()
    for copy in own:
        copy.start()
    for which in (1, 2, 3):
        for copy in copies[which]:
            copy.start()
    cot_pad[:, rows : 2 * rows, 0:cols] = cot[...]
    vel_out[:, rows : 2 * rows, 0:cols] = vel[...]
    for copy in copies[0]:
        copy.wait_recv()

    c = merge_border(cot_pad[...], 2)
    c0, c1 = c[0], c[1]
    rhs = -0.5 * ((roll_to(c0, -1, 0) - roll_to(c0, 1, 0)) + (roll_to(c1, -1, 1) - roll_to(c1, 1, 1)))
    fields = [rhs]
    for _ in range(ITERS):
        q = fields[-1]
        beside = roll_to(q, 2, 0) + roll_to(q, -2, 0) + roll_to(q, 2, 1)
        fields.append(-0.25 * (beside + roll_to(q, -2, 1)))
    inner = [f[rows : 2 * rows, 0:cols] for f in fields]
    partial = []
    for k in range(2 * ITERS):
        product = inner[k // 2] * inner[(k + 1) // 2]
        total = product[:, 0:128]
        for at_lane in range(128, cols, 128):
            total = total + product[:, at_lane : at_lane + 128]
        partial.append(jnp.sum(total, axis=0, keepdims=True))
    moments = jnp.concatenate(partial, axis=0)

    def share(slots, me, peers, count, send_s, recv_s, value):
        slots[me] = value
        started = []
        for k, peer in enumerate(peers):
            copy = pltpu.make_async_remote_copy(
                src_ref=slots.at[me], dst_ref=slots.at[me], send_sem=send_s.at[k], recv_sem=recv_s.at[k],
                device_id=peer, device_id_type=MESH,
            )
            copy.start()
            started.append(copy)
        for copy in started:
            copy.wait_recv()
        total = slots[0]
        for k in range(1, count):
            total = total + slots[k]
        for copy in started:
            copy.wait_send()
        return total

    moments = share(slots_y, gy, along_y, ny, send_y, recv_y, moments)
    moments = share(slots_x, gx, along_x, nx, send_x, recv_x, moments)
    moments = jnp.sum(moments, axis=1, keepdims=True)
    n = [moments[k : k + 1, 0:1] for k in range(2 * ITERS)]

    zero, one = jnp.zeros_like(n[0]), jnp.ones_like(n[0])
    lam, residual, direction = [zero] * (ITERS + 1), [one] + [zero] * ITERS, [one] + [zero] * ITERS
    norm_now = n[0]
    for step in range(ITERS):
        product = zero
        for i in range(step + 1):
            for j in range(step + 1):
                product = product + direction[i] * direction[j] * (n[i + j] + n[i + j + 1])
        alpha = norm_now / product
        lam = [x + alpha * p for x, p in zip(lam, direction)]
        if step + 1 < ITERS:
            image = [p + below for p, below in zip(direction, [zero] + direction[:-1])]
            residual = [r - alpha * a for r, a in zip(residual, image)]
            norm_next = zero
            for i in range(step + 2):
                for j in range(step + 2):
                    norm_next = norm_next + residual[i] * residual[j] * n[i + j]
            ratio = norm_next / norm_now
            direction = [r + ratio * p for r, p in zip(residual, direction)]
            norm_now = norm_next
    field = lam[0] * fields[0]
    for k in range(1, ITERS):
        field = field + lam[k] * fields[k]
    adj_out[0] = c0 + 0.5 * (roll_to(field, 1, 0) - roll_to(field, -1, 0))
    adj_out[1] = c1 + 0.5 * (roll_to(field, 1, 1) - roll_to(field, -1, 1))

    for copy in own:
        copy.wait()
    for which in (1, 2, 3):
        for copy in copies[which]:
            copy.wait_recv()
    for group in copies:
        for copy in group:
            copy.wait_send()


def conv_kernel(
    adj, vel, pad1, pad2, w_last, w_middle, w_first, spread_out, grads_out,
    adj_rolled, vel_rolled, stack, taps, deltas1, spread, gm, gl, gf,
):
    rows = spread_out.shape[1]
    cols = spread_out.shape[2]
    ch = w_middle.shape[0]
    v = merge_border(vel[...].astype(jnp.float32), 2)
    for b in (-1, 0, 1):
        for k in range(2):
            adj_rolled[2 * (b + 1) + k] = roll_to(adj[k], b, 1) if b else adj[k]
            vel_rolled[2 * (b + 1) + k] = roll_to(v[k], -b, 1) if b else v[k]
    spread[...] = jnp.zeros_like(spread)
    gm[...] = jnp.zeros_like(gm)
    gl[...] = jnp.zeros_like(gl)
    gf[...] = jnp.zeros_like(gf)
    taps[...] = jnp.zeros_like(taps)

    def gather(which, source, row, sign):
        for t in range(9):
            a, b = t // 3 - 1, t % 3 - 1
            for k in range(2):
                taps[which, 2 * t + k : 2 * t + k + 1, :] = source[2 * (b + 1) + k, pl.ds(row + sign * a, 1), :]

    def first(i, _):
        gather(0, adj_rolled, rows + i - 2, -1)
        shifted = taps[0].astype(jnp.bfloat16)
        pre = merge_border(pad2[i].astype(jnp.float32), 1)
        delta = dot(w_last[...], shifted, NN) * gelu_slope(pre)
        delta = delta.astype(jnp.bfloat16)
        wide = delta.astype(jnp.float32)
        base = pl.multiple_of(i * (3 * ch), 3 * ch)
        stack[pl.ds(base, ch), :] = roll_to(wide, -1, 1).astype(jnp.bfloat16)
        stack[pl.ds(base + ch, ch), :] = delta
        stack[pl.ds(base + 2 * ch, ch), :] = roll_to(wide, 1, 1).astype(jnp.bfloat16)
        return 0

    lax.fori_loop(0, rows + 4, first, 0)

    def second(j, _):
        base = pl.multiple_of(j * (3 * ch), 3 * ch)
        pre = merge_border(pad1[j].astype(jnp.float32), 1)
        delta = dot(w_middle[...], stack[pl.ds(base, 9 * ch), :], NN) * gelu_slope(pre)
        delta = delta.astype(jnp.bfloat16)
        deltas1[j] = delta
        e = dot(w_first[...], delta, NN)
        f = roll_to(e[0:8], -1, 1) + e[8:16] + roll_to(e[16:24], 1, 1)
        f = f[:, 0:cols]
        for a in (-1, 0, 1):
            for k in range(2):
                at = 2 * (a + 1) + k
                spread[k, pl.ds(j + 1 + a, 1), :] += f[at : at + 1, :]
        return 0

    lax.fori_loop(0, rows + 2, second, 0)

    ones_row = lax.broadcasted_iota(jnp.int32, (32, cols), 0) == 18

    def third(r, _):
        base = pl.multiple_of((r + 1) * (3 * ch), 3 * ch)
        hidden1 = gelu_value(pad1[r + 1][:, 0:cols].astype(jnp.float32)).astype(jnp.bfloat16)
        gm[...] += dot(stack[pl.ds(base, 9 * ch), 0:cols], hidden1, NT)
        hidden2 = gelu_value(pad2[r + 2][:, 0:cols].astype(jnp.float32)).astype(jnp.bfloat16)
        gather(0, adj_rolled, rows + r, -1)
        gl[...] += dot(taps[0][:, 0:cols].astype(jnp.bfloat16), hidden2, NT)
        gather(1, vel_rolled, rows + r, 1)
        taken = jnp.where(ones_row, 1.0, taps[1][:, 0:cols]).astype(jnp.bfloat16)
        delta2 = stack[pl.ds(base + 4 * ch, ch), 0:cols]
        both = jnp.concatenate([deltas1[r + 1][:, 0:cols], delta2], axis=0)
        gf[...] += dot(taken, both, NT)
        return 0

    lax.fori_loop(0, rows, third, 0)
    for k in range(2):
        spread_out[k] = adj[k, rows : 2 * rows, 0:cols] + spread[k, 2 : rows + 2, :]
    half = gm.shape[0] // 2
    grads_out[...] = jnp.zeros_like(grads_out)
    grads_out[0:half, 0:64] = gm[0:half]
    grads_out[0:half, 64:128] = gm[half:]
    ones = lax.broadcasted_iota(jnp.int32, (24, ch), 0) == 18
    grads_out[half : half + 24, 0:64] = gf[0:24, 0:ch]
    grads_out[half : half + 24, 64:128] = jnp.where(ones, gf[0:24, ch : 2 * ch], gl[0:24])


def reduce_kernel(nx, ny, factor, grads, out, slots_x, slots_y, send1, recv1, send2, recv2, send3, recv3):
    gx, gy, along_x, along_y = line_peers(nx, ny)
    greet(along_x + along_y)

    def copy(src, dst, send, recv, k, peer):
        made = pltpu.make_async_remote_copy(
            src_ref=src, dst_ref=dst, send_sem=send.at[k], recv_sem=recv.at[k], device_id=peer, device_id_type=MESH
        )
        made.start()
        return made

    first = [
        copy(grads.at[peer[0]], slots_x.at[gx], send1, recv1, k, peer) for k, peer in enumerate(along_x)
    ]
    slots_x[gx] = grads[gx]
    for c in first:
        c.wait_recv()
    total = slots_x[0]
    for k in range(1, nx):
        total = total + slots_x[k]
    slots_y[gy] = total
    second = [copy(slots_y.at[gy], slots_y.at[gy], send2, recv2, k, peer) for k, peer in enumerate(along_y)]
    for c in second:
        c.wait_recv()
    total = slots_y[0]
    for k in range(1, ny):
        total = total + slots_y[k]
    out[gx] = factor * total
    third = [copy(out.at[gx], out.at[gx], send3, recv3, k, peer) for k, peer in enumerate(along_x)]
    for c in third:
        c.wait_recv()
    for c in first + second + third:
        c.wait_send()


def per_device(nx, ny, cotangent, velocity_in, hidden_pre1, hidden_pre2, w_first, w_middle, w_last):
    rows, cols = cotangent.shape[1], cotangent.shape[2]
    ch = hidden_pre1.shape[0]
    f32, bf16 = jnp.float32, jnp.bfloat16
    factor = 1.0 / math.sqrt(rows * nx * cols * ny)
    vmem = pl.BlockSpec(memory_space=pltpu.VMEM)
    anywhere = pl.BlockSpec(memory_space=pl.ANY)
    dma = pltpu.SemaphoreType.DMA
    pre1 = jnp.transpose(hidden_pre1, (1, 0, 2))
    pre2 = jnp.transpose(hidden_pre2, (1, 0, 2))
    adj, vel, pad1, pad2 = pl.pallas_call(
        functools.partial(exchange_kernel, nx, ny),
        out_shape=(
            jax.ShapeDtypeStruct((2, 3 * rows, cols + 128), f32),
            jax.ShapeDtypeStruct((2, 3 * rows, cols + 256), bf16),
            jax.ShapeDtypeStruct((rows + 2, ch, cols + 256), bf16),
            jax.ShapeDtypeStruct((rows + 4, ch, cols + 256), bf16),
        ),
        in_specs=[vmem, vmem, anywhere, anywhere],
        out_specs=(vmem, vmem, anywhere, anywhere),
        scratch_shapes=[
            pltpu.VMEM((2, 3 * rows, cols + 256), f32),
            pltpu.VMEM((ny, 8, 128), f32),
            pltpu.VMEM((nx, 8, 128), f32),
            dma((4, 8)), dma((4, 8)), dma((2,)),
            dma((ny,)), dma((ny,)), dma((nx,)), dma((nx,)),
        ],
        compiler_params=pltpu.CompilerParams(collective_id=0, has_side_effects=True),
    )(cotangent, velocity_in, pre1, pre2)

    w_l = jnp.pad(w_last.reshape(18, ch), ((0, 14), (0, 0))).T
    w_m = w_middle.reshape(3, 3, ch, ch)[::-1].reshape(9 * ch, ch).T
    w_f = w_first.reshape(3, 3, ch, 2).transpose(1, 0, 3, 2).reshape(3, 6, ch)
    w_f = jnp.pad(w_f, ((0, 0), (0, 2), (0, 0))).reshape(24, ch)
    packed = 9 * ch // 2 + 24
    chunk = 8 * -(-packed // (8 * nx))
    grad_velocity, grads = pl.pallas_call(
        conv_kernel,
        out_shape=(
            jax.ShapeDtypeStruct((2, rows, cols), f32),
            jax.ShapeDtypeStruct((nx * chunk, 128), f32),
        ),
        in_specs=[vmem] * 7,
        out_specs=(vmem, vmem),
        scratch_shapes=[
            pltpu.VMEM((6, 3 * rows, cols + 128), f32),
            pltpu.VMEM((6, 3 * rows, cols + 128), f32),
            pltpu.VMEM(((rows + 4) * 3 * ch, cols + 128), bf16),
            pltpu.VMEM((2, 32, cols + 128), f32),
            pltpu.VMEM((rows + 2, ch, cols + 128), bf16),
            pltpu.VMEM((2, rows + 8, cols), f32),
            pltpu.VMEM((9 * ch, ch), f32),
            pltpu.VMEM((32, ch), f32),
            pltpu.VMEM((32, 2 * ch), f32),
        ],
        compiler_params=pltpu.CompilerParams(vmem_limit_bytes=48 * 2**20),
    )(adj, vel, pad1, pad2, w_l, w_m, w_f)

    summed = pl.pallas_call(
        functools.partial(reduce_kernel, nx, ny, factor),
        out_shape=jax.ShapeDtypeStruct((nx, chunk, 128), f32),
        in_specs=[vmem],
        out_specs=vmem,
        scratch_shapes=[
            pltpu.VMEM((nx, chunk, 128), f32),
            pltpu.VMEM((ny, chunk, 128), f32),
            dma((nx,)), dma((nx,)), dma((ny,)), dma((ny,)), dma((nx,)), dma((nx,)),
        ],
        compiler_params=pltpu.CompilerParams(collective_id=1, has_side_effects=True),
    )(grads.reshape(nx, chunk, 128))
    summed = summed.reshape(nx * chunk, 128)
    half = 9 * ch // 2
    middle = jnp.concatenate([summed[:half, :ch], summed[:half, ch:]], axis=0)
    middle = middle.reshape(3, 3, ch, ch)[::-1].reshape(9, ch, ch)
    small = summed[half : half + 24]
    grad_first = small[:18, :ch].reshape(9, 2, ch).transpose(0, 2, 1)
    grad_last = small[:18, ch:].reshape(9, 2, ch)
    return grad_velocity, grad_first, middle, grad_last, small[18, :ch], small[18, ch:]


def solution(mesh):
    whole = P(None, "gx", "gy")
    return jax.shard_map(
        functools.partial(per_device, mesh.shape["gx"], mesh.shape["gy"]),
        mesh=mesh,
        in_specs=(whole, whole, whole, whole, P(), P(), P()),
        out_specs=(whole, P(), P(), P(), P(), P()),
        check_vma=False,
    )
```

time: 424 us -> 109 us (0.26)
  blocking collectives: 204 us -> 0 us
  Pallas kernels: 0 us -> 93.7 us
  waiting for transfers between devices: 90.2 us -> 0 us
  starting transfers between devices: 46.5 us -> 0 us
  between operations: 28.6 us -> 0.74 us
  matrix products: 23.8 us -> 0 us
  other arithmetic: 15.2 us -> 0.02 us
    psum x5 -> x0, blocking collectives: 204 us -> none  [the longest x4 164 us: paired_sums(): lax.psum((jnp.sum(residual * residual), jnp.sum(residual * image)), ('gx'...]
    pallas_call x0 -> x3, Pallas kernels: none -> 93.7 us  [the longest x1 57.6 us: per_device(): pl.pallas_call(functools.partial(exchange_kernel, nx, ny), out_shape=(jax...]
    psum x1 -> x0, waiting for transfers between devices: 60.6 us -> none  [per_device(): lax.psum((grad_first, grad_middle, grad_last, bias_one, bias_two), ('gx',...]
    ppermute x28 -> x0, starting transfers between devices: 46.5 us -> none  [the longest x14 29.5 us: with_halo(): after = lax.ppermute(leading, axis, down)]
    ppermute x28 -> x0, waiting for transfers between devices: 29.6 us -> none  [the longest x14 23.7 us: with_halo(): before = lax.ppermute(last, axis, up)]
    dot_general x54 -> x0, matrix products: 23.8 us -> none  [the longest x27 14.4 us: grads_from_padded_deltas(): lax.dot_general(shifted, flat_inputs, (((1,), (1,)), ((), ())), preferred...]
    reduce_sum x6 -> x0, other arithmetic: 5.41 us -> none  [the longest x4 2.79 us: paired_sums(): jnp.sum(residual * image)]
    mul x6 -> x0, other arithmetic: 4.84 us -> none  [the longest x1 1.7 us: per_device(): factor * summed[1]]
  transfers between devices with their start and end apart: 29 -> 0, of which waited for: 18 -> 0; matrix products, arithmetic and copies ran while one was open for 5% -> 0% of each run, Pallas kernels for 0% -> 0%
where the time goes in v1:
time: 109 us; the launch traced here: 108 us
  Pallas kernels  93.7 us (86%)
  local copies, waits for them, and re-layouts  13.8 us (13%)
    pallas_call x1, Pallas kernels, per_device(): pl.pallas_call(functools.partial(exchange_kernel, nx, ny), out_shape=(jax...  57.6 us
    pallas_call x1, Pallas kernels, per_device(): pl.pallas_call(conv_kernel, out_shape=(jax.ShapeDtypeStruct((2, rows, col...  19.5 us
    pallas_call x1, Pallas kernels, per_device(): pl.pallas_call(functools.partial(reduce_kernel, nx, ny, factor), out_shap...  16.5 us
    unnamed x16, local copies, waits for them, and re-layouts  5.3 us
    transpose x1, local copies, waits for them, and re-layouts, per_device(): pre2 = jnp.transpose(hidden_pre2, (1, 0, 2))  2.94 us

profile of v1, /device:TPU:0, one launch (start us, length us, event | category | flops | bytes accessed | tf_op | source)
XLA Modules:
  0.0 108.2 jit_solution(1820511083989961066)
XLA Ops:
  0.6 0.0 copy-start.5
  0.6 2.9 %copy_bitcast_fusion = (bf16[16,64,384]{2,1,0:T(8,128)(2,1)}, bf16[16,64,384]{2,1,0:T(8,128)(2,1)}) fusion(bf16[64,16,384]{2,1,0:T(8,128)(2,1)} %param.10, bf16[64,16,384]{2,1,0:T(8,128)(2,1)} %param.9), kind=kLoop, calls=%fused_computation | loop fusion | bytes 3145728 | tf_op jit(solution)/shard_map/transpose | solution.py:318
  3.6 0.0 copy-start.7
  3.6 0.0 copy-start.6
  3.6 57.6 %shard_map.118 = (f32[2,48,512]{2,1,0:T(8,128)}, bf16[2,48,640]{2,1,0:T(8,128)(2,1)}, bf16[18,64,640]{2,1,0:T(8,128)(2,1)}, bf16[20,64,640]{2,1,0:T(8,128)(2,1)}) custom-call(f32[2,16,384]{2,1,0:T(8,128)} %cot.1, bf16[2,16,384]{2,1,0:T(8,128)(2,1)} %vel.1, bf16[16,64,384]{2,1,0:T(8,128)(2,1)} %get-tuple-element.25.pre1, ...), custom_call_target="tpu_custom_call" | custom-call | tf_op jit(solution)/shard_map/pallas_call | solution.py:319
  61.2 0.0 copy-done.5
  61.2 0.1 copy.21
  61.4 0.0 copy-done.7
  61.4 0.1 copy.20
  61.5 0.0 copy-done.6
  61.6 0.0 copy-start
  61.6 1.4 %copy-done = bf16[20,64,640]{2,1,0:T(8,128)(2,1)S(1)} copy-done((bf16[20,64,640]{2,1,0:T(8,128)(2,1)S(1)}, bf16[20,64,640]{2,1,0:T(8,128)(2,1)}, u32[]{:S(2)}) %copy-start) | copy-done | bytes 1638424
  63.0 0.0 copy-start.1
  63.0 1.4 %copy-done.1 = bf16[18,64,640]{2,1,0:T(8,128)(2,1)S(1)} copy-done((bf16[18,64,640]{2,1,0:T(8,128)(2,1)S(1)}, bf16[18,64,640]{2,1,0:T(8,128)(2,1)}, u32[]{:S(2)}) %copy-start.1) | copy-done | bytes 1474584
  64.4 0.0 copy-start.2
  64.4 0.9 copy-done.2
  65.3 0.0 copy-start.4
  65.3 0.9 copy-done.4
  66.2 19.5 %shard_map.119 = (f32[2,16,384]{2,1,0:T(8,128)}, f32[320,128]{1,0:T(8,128)S(1)}) custom-call(f32[2,48,512]{2,1,0:T(8,128)S(1)} %copy-done.2, bf16[2,48,640]{2,1,0:T(8,128)(2,1)S(1)} %copy-done.4, bf16[18,64,640]{2,1,0:T(8,128)(2,1)S(1)} %copy-done.1, bf16[20,64,640]{2,1,0:T(8,128)(2,1)S(1)} %copy-done, bf16[64,32]{1,0:T(8,128)(2,1)S(1)} %pad_bitcast_fusion.w_last, ...), custom_call_target="tpu_custom_call" | custom-call | tf_op jit(solution)/shard_map/pallas_call | solution.py:345
  85.7 0.0 copy-start.3
  85.7 0.7 copy-done.3
  86.4 16.5 %shard_map.120 = f32[8,40,128]{2,1,0:T(8,128)} custom-call(f32[8,40,128]{2,1,0:T(8,128)} %bitcast.24), custom_call_target="tpu_custom_call" | custom-call | tf_op jit(solution)/shard_map/pallas_call | solution.py:367
  102.9 1.1 fusion.1
  104.1 0.7 rev.7
  104.8 0.9 fusion
  105.7 0.6 reshape.56
  106.3 0.6 reshape.59
  106.9 1.3 %slice_bitcast_fusion = (f32[64]{0:T(128)}, f32[64]{0:T(128)}) fusion(f32[320,128]{1,0:T(8,128)} %bitcast.27), kind=kLoop, calls=%fused_computation.5 | loop fusion | bytes 1024 | tf_op jit(solution)/shard_map/squeeze | solution.py:386
  (7 shorter events, 0.1 us)
Async XLA Ops:
  0.6 60.6 %copy-start.5 = (bf16[9,64,64]{2,1,0:T(8,128)(2,1)S(1)}, bf16[9,64,64]{2,1,0:T(8,128)(2,1)}, u32[]{:S(2)}) copy-start(bf16[9,64,64]{2,1,0:T(8,128)(2,1)} %param.12) | copy-start | bytes 221188
  3.6 57.8 %copy-start.7 = (bf16[9,2,64]{2,1,0:T(2,128)(2,1)S(1)}, bf16[9,2,64]{2,1,0:T(2,128)(2,1)}, u32[]{:S(2)}) copy-start(bf16[9,2,64]{2,1,0:T(2,128)(2,1)} %param.13) | copy-start | bytes 6916
  3.6 57.9 %copy-start.6 = (bf16[9,64,2]{1,2,0:T(2,128)(2,1)S(1)}, bf16[9,64,2]{1,2,0:T(2,128)(2,1)}, u32[]{:S(2)}) copy-start(bf16[9,64,2]{1,2,0:T(2,128)(2,1)} %param.11) | copy-start | bytes 6916
  61.6 1.4 %copy-start = (bf16[20,64,640]{2,1,0:T(8,128)(2,1)S(1)}, bf16[20,64,640]{2,1,0:T(8,128)(2,1)}, u32[]{:S(2)}) copy-start(bf16[20,64,640]{2,1,0:T(8,128)(2,1)} %get-tuple-element.15.pad2) | copy-start | bytes 4915204
  63.0 1.4 %copy-start.1 = (bf16[18,64,640]{2,1,0:T(8,128)(2,1)S(1)}, bf16[18,64,640]{2,1,0:T(8,128)(2,1)}, u32[]{:S(2)}) copy-start(bf16[18,64,640]{2,1,0:T(8,128)(2,1)} %get-tuple-element.14.pad1) | copy-start | bytes 4423684
  64.4 0.9 copy-start.2
  65.3 0.9 copy-start.4
  85.7 0.7 copy-start.3

commit v2 on v1

v2 whole, which is shorter than its diff:
```python
import functools
import math

import jax
import jax.numpy as jnp
from jax import lax
from jax.experimental import pallas as pl
from jax.experimental.pallas import tpu as pltpu
from jax.sharding import PartitionSpec as P

ITERS = 4
MESH = pl.DeviceIdType.MESH
NEIGHBOURS = tuple((dx, dy) for dx in (-1, 0, 1) for dy in (-1, 0, 1) if (dx, dy) != (0, 0))
NT = (((1,), (1,)), ((), ()))
NN = (((1,), (0,)), ((), ()))
C0 = 0.7978845608028654
C1 = 0.044715


def dot(a, b, dims):
    return lax.dot_general(a, b, dims, preferred_element_type=jnp.float32)


def roll_to(x, shift, axis):
    return pltpu.roll(x, shift % x.shape[axis], axis)


def gelu_both(v):
    square = v * v
    half = 0.5 * (1.0 + jnp.tanh(v * (C0 + (C0 * C1) * square)))
    value = v * half
    return value, half + (value * (1.0 - half)) * (2.0 * C0 + (6.0 * C0 * C1) * square)


def greet(peers):
    barrier = pltpu.get_barrier_semaphore()
    for peer in peers:
        pl.semaphore_signal(barrier, inc=1, device_id=peer, device_id_type=MESH)
    pl.semaphore_wait(barrier, len(peers))


def line_peers(nx, ny):
    gx, gy = lax.axis_index("gx"), lax.axis_index("gy")
    along_x = [(lax.rem(gx + k, nx), gy) for k in range(1, nx)]
    along_y = [(gx, lax.rem(gy + k, ny)) for k in range(1, ny)]
    return gx, gy, along_x, along_y


def merge_border(block, axis):
    n = block.shape[axis] - 256
    right = lax.slice_in_dim(block, n, n + 128, axis=axis)
    left = lax.slice_in_dim(block, n + 128, n + 256, axis=axis)
    lane = lax.broadcasted_iota(jnp.int32, right.shape, axis)
    border = jnp.where(lane < 64, right, left)
    return jnp.concatenate([lax.slice_in_dim(block, 0, n, axis=axis), border], axis=axis)


def fused_kernel(
    nx, ny, factor, cot, vel, pre1, pre2, edges, w_last, w_middle, w_first,
    spread_out, middle_out, last_out, small_out,
    cot_pad, vel_pad, edge_in, halo1, halo2, slots_y, slots_x, grads, sums_x, sums_y, gathered, few_y, few_x,
    adj, adj_rolled, vel_rolled, slope1, slope2, hidden1, hidden2, stack, taps, spread, gm, gl, gf,
    send, recv, send_y, recv_y, send_x, recv_x,
):
    rows, cols = cot.shape[1], cot.shape[2]
    ch = pre1.shape[1]
    f32, bf16 = jnp.float32, jnp.bfloat16
    gx, gy, along_x, along_y = line_peers(nx, ny)

    def at(dx, dy):
        return (lax.rem(gx + dx + nx, nx), lax.rem(gy + dy + ny, ny))

    corners = [at(dx, dy) for dx, dy in NEIGHBOURS if dx and dy]
    greet(along_x + along_y + corners)

    def remote(src, dst, which, index, peer):
        return pltpu.make_async_remote_copy(
            src_ref=src, dst_ref=dst, send_sem=send.at[which, index], recv_sem=recv.at[which, index],
            device_id=peer, device_id_type=MESH,
        )

    def block_copy(src, dst, which, index, dx, dy):
        t = rows * (1 - dx)
        lanes = {1: slice(cols - 128, cols), 0: slice(0, cols), -1: slice(0, 128)}[dy]
        land = {1: slice(cols + 128, cols + 256), 0: slice(0, cols), -1: slice(cols, cols + 128)}[dy]
        return remote(src.at[:, :, lanes], dst.at[:, t : t + rows, land], which, index, at(dx, dy))

    cot_copies = [block_copy(cot, cot_pad, 0, i, dx, dy) for i, (dx, dy) in enumerate(NEIGHBOURS)]
    vel_copies = [block_copy(vel, vel_pad, 1, i, dx, dy) for i, (dx, dy) in enumerate(NEIGHBOURS)]
    edge_copies = [
        remote(edges.at[(1 + dy) // 2], edge_in.at[(1 + dy) // 2, 1 - dx], 2, i, at(dx, dy))
        for i, (dx, dy) in enumerate(NEIGHBOURS) if dy
    ]
    row_copies = [
        remote(pre2.at[rows - 2 : rows], halo2.at[0:2], 3, 0, at(1, 0)),
        remote(pre2.at[0:2], halo2.at[2:4], 3, 1, at(-1, 0)),
        remote(pre1.at[rows - 1 : rows], halo1.at[0:1], 3, 2, at(1, 0)),
        remote(pre1.at[0:1], halo1.at[1:2], 3, 3, at(-1, 0)),
    ]
    for copy in cot_copies + edge_copies + row_copies + vel_copies:
        copy.start()
    cot_pad[:, rows : 2 * rows, 0:cols] = cot[...]
    vel_pad[:, rows : 2 * rows, 0:cols] = vel[...]
    spread[...] = jnp.zeros_like(spread)
    gm[...] = jnp.zeros_like(gm)
    gl[...] = jnp.zeros_like(gl)
    gf[...] = jnp.zeros_like(gf)
    taps[...] = jnp.zeros_like(taps)

    def activate(r, _):
        value, slope = gelu_both(pre2[r].astype(f32))
        hidden2[r] = value.astype(bf16)
        slope2[r + 2, :, 0:cols] = slope
        value, slope = gelu_both(pre1[r].astype(f32))
        hidden1[r] = value.astype(bf16)
        slope1[r + 1, :, 0:cols] = slope
        return 0

    for copy in cot_copies:
        copy.wait_recv()
    c = merge_border(cot_pad[...], 2)
    c0, c1 = c[0], c[1]
    rhs = -0.5 * ((roll_to(c0, -1, 0) - roll_to(c0, 1, 0)) + (roll_to(c1, -1, 1) - roll_to(c1, 1, 1)))
    fields = [rhs]
    for _ in range(ITERS):
        q = fields[-1]
        beside = roll_to(q, 2, 0) + roll_to(q, -2, 0) + roll_to(q, 2, 1)
        fields.append(-0.25 * (beside + roll_to(q, -2, 1)))
    inner = [f[rows : 2 * rows, 0:cols] for f in fields]
    partial = []
    for k in range(2 * ITERS):
        product = inner[k // 2] * inner[(k + 1) // 2]
        total = product[:, 0:128]
        for at_lane in range(128, cols, 128):
            total = total + product[:, at_lane : at_lane + 128]
        partial.append(jnp.sum(total, axis=0, keepdims=True))
    moments = jnp.concatenate(partial, axis=0)

    def begin(slots, me, peers, sems, which):
        started = []
        for k, peer in enumerate(peers):
            copy = pltpu.make_async_remote_copy(
                src_ref=slots.at[me], dst_ref=slots.at[me], send_sem=sems[0].at[which, k],
                recv_sem=sems[1].at[which, k], device_id=peer, device_id_type=MESH,
            )
            copy.start()
            started.append(copy)
        return started

    def finish(slots, count, started):
        for copy in started:
            copy.wait_recv()
        total = slots[0]
        for k in range(1, count):
            total = total + slots[k]
        for copy in started:
            copy.wait_send()
        return total

    sems_y, sems_x = (send_y, recv_y), (send_x, recv_x)
    slots_y[gy] = moments
    started = begin(slots_y, gy, along_y, sems_y, 0)
    lax.fori_loop(0, rows // 2, activate, 0)
    slots_x[gx] = finish(slots_y, ny, started)
    started = begin(slots_x, gx, along_x, sems_x, 0)
    lax.fori_loop(rows // 2, rows, activate, 0)

    for copy in row_copies + edge_copies:
        copy.wait_recv()
    lane = lax.broadcasted_iota(jnp.int32, (ch, 128), 1)
    place = lax.rem(lane, 64)
    top = place < jnp.where(lane < 64, 4, 2)
    bottom = place >= jnp.where(lane < 64, 36, 34)
    sides = []
    for side in range(2):
        mid = jnp.where(top, pltpu.roll(edge_in[side, 0], 96, 1), edge_in[side, 1])
        sides.append(jnp.where(bottom, pltpu.roll(edge_in[side, 2], 32, 1), mid))

    def edge_slope(offset):
        right = pltpu.roll(sides[0], lax.rem(256 - offset, 128), 1)
        left = pltpu.roll(sides[1], lax.rem(254 - offset, 128), 1)
        return gelu_both(jnp.where(lane < 64, right, left))[1]

    def edge2(i, _):
        slope2[i, :, cols : cols + 128] = edge_slope(2 * i)
        return 0

    def edge1(j, _):
        slope1[j, :, cols : cols + 128] = edge_slope(64 + 2 * j)
        return 0

    lax.fori_loop(0, rows + 4, edge2, 0)
    lax.fori_loop(0, rows + 2, edge1, 0)
    for i, row in enumerate((0, 1, rows + 2, rows + 3)):
        slope2[row, :, 0:cols] = gelu_both(halo2[i].astype(f32))[1]
    for i, row in enumerate((0, rows + 1)):
        slope1[row, :, 0:cols] = gelu_both(halo1[i].astype(f32))[1]
    for copy in vel_copies:
        copy.wait_recv()
    v = merge_border(vel_pad[...].astype(f32), 2)
    for b in (-1, 0, 1):
        for k in range(2):
            vel_rolled[2 * (b + 1) + k] = roll_to(v[k], -b, 1) if b else v[k]

    moments = jnp.sum(finish(slots_x, nx, started), axis=1, keepdims=True)
    n = [moments[k : k + 1, 0:1] for k in range(2 * ITERS)]
    zero, one = jnp.zeros_like(n[0]), jnp.ones_like(n[0])
    lam, residual, direction = [zero] * (ITERS + 1), [one] + [zero] * ITERS, [one] + [zero] * ITERS
    norm_now = n[0]
    for step in range(ITERS):
        product = zero
        for i in range(step + 1):
            for j in range(step + 1):
                product = product + direction[i] * direction[j] * (n[i + j] + n[i + j + 1])
        alpha = norm_now / product
        lam = [x + alpha * p for x, p in zip(lam, direction)]
        if step + 1 < ITERS:
            image = [p + below for p, below in zip(direction, [zero] + direction[:-1])]
            residual = [r - alpha * a for r, a in zip(residual, image)]
            norm_next = zero
            for i in range(step + 2):
                for j in range(step + 2):
                    norm_next = norm_next + residual[i] * residual[j] * n[i + j]
            ratio = norm_next / norm_now
            direction = [r + ratio * p for r, p in zip(residual, direction)]
            norm_now = norm_next
    field = lam[0] * fields[0]
    for k in range(1, ITERS):
        field = field + lam[k] * fields[k]
    adj[0] = c0 + 0.5 * (roll_to(field, 1, 0) - roll_to(field, -1, 0))
    adj[1] = c1 + 0.5 * (roll_to(field, 1, 1) - roll_to(field, -1, 1))
    for b in (-1, 0, 1):
        for k in range(2):
            adj_rolled[2 * (b + 1) + k] = roll_to(adj[k], b, 1) if b else adj[k]

    def gather(which, source, row, sign):
        for t in range(9):
            a, b = t // 3 - 1, t % 3 - 1
            for k in range(2):
                taps[which, 2 * t + k : 2 * t + k + 1, :] = source[2 * (b + 1) + k, pl.ds(row + sign * a, 1), :]

    def first(i, own):
        gather(0, adj_rolled, rows + i - 2, -1)
        shifted = taps[0].astype(bf16)
        delta = (dot(w_last[...], shifted, NN) * slope2[i]).astype(bf16)
        wide = delta.astype(f32)
        base = pl.multiple_of(i * (3 * ch), 3 * ch)
        stack[pl.ds(base, ch), :] = roll_to(wide, -1, 1).astype(bf16)
        stack[pl.ds(base + ch, ch), :] = delta
        stack[pl.ds(base + 2 * ch, ch), :] = roll_to(wide, 1, 1).astype(bf16)
        if own:
            gl[...] += dot(shifted[:, 0:cols], hidden2[i - 2], NT)
        return 0

    for low, high, own in ((0, 2, False), (2, rows + 2, True), (rows + 2, rows + 4, False)):
        lax.fori_loop(low, high, lambda i, _, own=own: first(i, own), 0)

    def middle(r, _):
        base = pl.multiple_of((r + 1) * (3 * ch), 3 * ch)
        gm[...] += dot(stack[pl.ds(base, 9 * ch), 0:cols], hidden1[r], NT)
        return 0

    lax.fori_loop(0, rows, middle, 0)
    half = 9 * ch // 2
    chunk = grads.shape[1]
    total_rows = nx * chunk
    lower = jnp.concatenate([gl[0:24], jnp.zeros((24, ch), f32)], axis=1)
    packed = jnp.concatenate([gm[0:half], gm[half : 2 * half]], axis=1)
    packed = jnp.concatenate([packed, lower, jnp.zeros((total_rows - half - 24, 128), f32)], axis=0)
    for k in range(nx):
        grads[k] = packed[k * chunk : (k + 1) * chunk]
    scatter = [
        pltpu.make_async_remote_copy(
            src_ref=grads.at[peer[0]], dst_ref=sums_x.at[gx], send_sem=send_x.at[1, k], recv_sem=recv_x.at[1, k],
            device_id=peer, device_id_type=MESH,
        )
        for k, peer in enumerate(along_x)
    ]
    for copy in scatter:
        copy.start()
    sums_x[gx] = grads[gx]

    ones_row = lax.broadcasted_iota(jnp.int32, (32, cols), 0) == 18

    def second(j, own):
        base = pl.multiple_of(j * (3 * ch), 3 * ch)
        delta = dot(w_middle[...], stack[pl.ds(base, 9 * ch), :], NN) * slope1[j]
        delta = delta.astype(bf16)
        e = dot(w_first[...], delta, NN)
        f = roll_to(e[0:8], -1, 1) + e[8:16] + roll_to(e[16:24], 1, 1)
        f = f[:, 0:cols]
        for a in (-1, 0, 1):
            for k in range(2):
                row = 2 * (a + 1) + k
                spread[k, pl.ds(j + 1 + a, 1), :] += f[row : row + 1, :]
        if own:
            gather(1, vel_rolled, rows + j - 1, 1)
            taken = jnp.where(ones_row, 1.0, taps[1][:, 0:cols]).astype(bf16)
            delta2 = stack[pl.ds(base + 4 * ch, ch), 0:cols]
            gf[...] += dot(taken, jnp.concatenate([delta[:, 0:cols], delta2], axis=0), NT)
        return 0

    half_way = rows // 2 + 1
    second(0, False)
    lax.fori_loop(1, half_way, lambda j, _: second(j, True), 0)
    sums_y[gy] = finish(sums_x, nx, scatter)
    started = begin(sums_y, gy, along_y, sems_y, 1)
    lax.fori_loop(half_way, rows + 1, lambda j, _: second(j, True), 0)
    few_y[gy] = gf[0:24]
    few = begin(few_y, gy, along_y, sems_y, 2)
    gathered[gx] = factor * finish(sums_y, ny, started)
    spreading = begin(gathered, gx, along_x, sems_x, 2)
    few_x[gx] = finish(few_y, ny, few)
    few = begin(few_x, gx, along_x, sems_x, 3)
    second(rows + 1, False)
    for k in range(2):
        spread_out[k] = adj[k, rows : 2 * rows, 0:cols] + spread[k, 2 : rows + 2, :]
    for copy in cot_copies + edge_copies + row_copies + vel_copies:
        copy.wait_send()
    for copy in spreading:
        copy.wait_recv()
    for copy in spreading:
        copy.wait_send()
    whole = jnp.concatenate([gathered[k] for k in range(nx)], axis=0)
    for place_at in range(9):
        t = 3 * (2 - place_at // 3) + place_at % 3
        start = place_at * ch
        for low in range(0, ch, 32):
            here = start + low
            side = 0 if here < half else 64
            here = here % half
            middle_out[t, low : low + 32, :] = whole[here : here + 32, side : side + ch]
    for t in range(9):
        last_out[t] = whole[half + 2 * t : half + 2 * t + 2, 0:ch]
    small_out[...] = factor * finish(few_x, nx, few)


def per_device(nx, ny, cotangent, velocity_in, hidden_pre1, hidden_pre2, w_first, w_middle, w_last):
    rows, cols = cotangent.shape[1], cotangent.shape[2]
    ch = hidden_pre1.shape[0]
    f32, bf16 = jnp.float32, jnp.bfloat16
    factor = 1.0 / math.sqrt(rows * nx * cols * ny)
    vmem = pl.BlockSpec(memory_space=pltpu.VMEM)
    dma = pltpu.SemaphoreType.DMA
    pre1 = jnp.transpose(hidden_pre1, (1, 0, 2))
    pre2 = jnp.transpose(hidden_pre2, (1, 0, 2))

    def edge(low):
        first = hidden_pre1[:, :, low : low + 2].reshape(ch, 2 * rows).astype(f32)
        second = hidden_pre2[:, :, low : low + 2].reshape(ch, 2 * rows).astype(f32)
        return jnp.pad(second, ((0, 0), (4, 124 - 2 * rows))) + jnp.pad(first, ((0, 0), (66, 62 - 2 * rows)))

    edges = jnp.stack([edge(0), edge(cols - 2)])
    w_l = jnp.pad(w_last.reshape(18, ch), ((0, 14), (0, 0))).T
    w_m = w_middle.reshape(3, 3, ch, ch)[::-1].reshape(9 * ch, ch).T
    w_f = w_first.reshape(3, 3, ch, 2).transpose(1, 0, 3, 2).reshape(3, 6, ch)
    w_f = jnp.pad(w_f, ((0, 0), (0, 2), (0, 0))).reshape(24, ch)
    packed = 9 * ch // 2 + 24
    chunk = 8 * -(-packed // (8 * nx))
    wide = cols + 128
    most = max(8, nx, ny)
    grad_velocity, grad_middle, grad_last, small = pl.pallas_call(
        functools.partial(fused_kernel, nx, ny, factor),
        out_shape=(
            jax.ShapeDtypeStruct((2, rows, cols), f32),
            jax.ShapeDtypeStruct((9, ch, ch), f32),
            jax.ShapeDtypeStruct((9, 2, ch), f32),
            jax.ShapeDtypeStruct((24, 128), f32),
        ),
        in_specs=[vmem] * 8,
        out_specs=(vmem,) * 4,
        scratch_shapes=[
            pltpu.VMEM((2, 3 * rows, cols + 256), f32),
            pltpu.VMEM((2, 3 * rows, cols + 256), bf16),
            pltpu.VMEM((2, 3, ch, 128), f32),
            pltpu.VMEM((2, ch, cols), bf16),
            pltpu.VMEM((4, ch, cols), bf16),
            pltpu.VMEM((ny, 8, 128), f32),
            pltpu.VMEM((nx, 8, 128), f32),
            pltpu.VMEM((nx, chunk, 128), f32),
            pltpu.VMEM((nx, chunk, 128), f32),
            pltpu.VMEM((ny, chunk, 128), f32),
            pltpu.VMEM((nx, chunk, 128), f32),
            pltpu.VMEM((ny, 24, 128), f32),
            pltpu.VMEM((nx, 24, 128), f32),
            pltpu.VMEM((2, 3 * rows, wide), f32),
            pltpu.VMEM((6, 3 * rows, wide), f32),
            pltpu.VMEM((6, 3 * rows, wide), f32),
            pltpu.VMEM((rows + 2, ch, wide), f32),
            pltpu.VMEM((rows + 4, ch, wide), f32),
            pltpu.VMEM((rows, ch, cols), bf16),
            pltpu.VMEM((rows, ch, cols), bf16),
            pltpu.VMEM(((rows + 4) * 3 * ch, wide), bf16),
            pltpu.VMEM((2, 32, wide), f32),
            pltpu.VMEM((2, rows + 8, cols), f32),
            pltpu.VMEM((9 * ch, ch), f32),
            pltpu.VMEM((32, ch), f32),
            pltpu.VMEM((32, 2 * ch), f32),
            dma((4, 8)), dma((4, 8)),
            dma((3, ny)), dma((3, ny)), dma((4, nx)), dma((4, nx)),
        ],
        compiler_params=pltpu.CompilerParams(
            collective_id=0, has_side_effects=True, vmem_limit_bytes=48 * 2**20
        ),
    )(cotangent, velocity_in, pre1, pre2, edges, w_l, w_m, w_f)
    grad_first = small[:18, :ch].reshape(9, 2, ch).transpose(0, 2, 1)
    return grad_velocity, grad_first, grad_middle, grad_last, small[18, :ch], small[18, ch:]


def solution(mesh):
    whole = P(None, "gx", "gy")
    return jax.shard_map(
        functools.partial(per_device, mesh.shape["gx"], mesh.shape["gy"]),
        mesh=mesh,
        in_specs=(whole, whole, whole, whole, P(), P(), P()),
        out_specs=(whole, P(), P(), P(), P(), P()),
        check_vma=False,
    )
```

time: 109 us -> 64 us (0.59)
  Pallas kernels: 93.7 us -> 53.4 us
  local copies, waits for them, and re-layouts: 13.8 us -> 9.52 us
    pallas_call x3 -> x1, Pallas kernels: 93.7 us -> 53.4 us  [per_device(): pl.pallas_call(functools.partial(fused_kernel, nx, ny, factor), out_shape...]
    transpose x1, local copies, waits for them, and re-layouts: 2.94 us -> 0.37 us  [per_device(): pre2 = jnp.transpose(hidden_pre2, (1, 0, 2))]
    unnamed x16 -> x13, local copies, waits for them, and re-layouts: 5.3 us -> 3.13 us
    slice x2 -> x6, local copies, waits for them, and re-layouts: 1.93 us -> 2.51 us  [the longest x3 1.81 us: edge(): first = hidden_pre1[:, :, low:low + 2].reshape(ch, 2 * rows).astype(f32)]
where the time goes in v2:
time: 64 us; the launch traced here: 63.7 us
  Pallas kernels  53.4 us (83%)
  local copies, waits for them, and re-layouts  9.52 us (15%)
  between operations  0.73 us (1%)
    pallas_call x1, Pallas kernels, per_device(): pl.pallas_call(functools.partial(fused_kernel, nx, ny, factor), out_shape...  53.4 us
    unnamed x13, local copies, waits for them, and re-layouts  3.13 us
    slice x3, local copies, waits for them, and re-layouts, edge(): first = hidden_pre1[:, :, low:low + 2].reshape(ch, 2 * rows).astype(f32)  1.81 us

profile of v2, /device:TPU:0, one launch (start us, length us, event | category | flops | bytes accessed | tf_op | source)
XLA Modules:
  0.0 63.7 jit_solution(12576969100131591258)
XLA Ops:
  0.6 0.7 %copy.30 = bf16[3,3,2,64]{3,2,1,0:T(2,128)(2,1)S(1)} copy(bf16[3,3,2,64]{3,2,0,1:T(2,128)(2,1)} %bitcast.37) | data formatting | bytes 4608 | tf_op jit(solution)/shard_map/transpose | solution.py:356
  1.3 0.0 copy-start.4
  1.4 0.7 %copy-done.4 = bf16[9,2,64]{2,1,0:T(2,128)(2,1)S(1)} copy-done((bf16[9,2,64]{2,1,0:T(2,128)(2,1)S(1)}, bf16[9,2,64]{2,1,0:T(2,128)(2,1)}, u32[]{:S(2)}) %copy-start.4) | copy-done | bytes 2328
  2.1 0.1 copy.28
  2.2 0.9 %rev.3 = bf16[3,3,64,64]{3,2,1,0:T(8,128)(2,1)S(1)} reverse(bf16[3,3,64,64]{3,2,1,0:T(8,128)(2,1)} %bitcast.31), dimensions={0} | reverse | bytes 147456 | tf_op jit(solution)/shard_map/rev | solution.py:355
  3.1 0.1 copy.29
  3.2 0.0 copy-start.2
  3.3 1.2 %fusion.1 = (bf16[64,16,2]{2,1,0:T(8,128)(2,1)S(1)}, bf16[64,16,2]{2,1,0:T(8,128)(2,1)S(1)}) fusion(bf16[64,16,384]{2,1,0:T(8,128)(2,1)} %param.9), kind=kLoop, calls=%fused_computation.10 | loop fusion | bytes 16384 | tf_op jit(solution)/shard_map/slice | solution.py:349
  4.5 0.3 copy.22
  4.8 0.1 copy.23
  4.9 0.3 copy.26
  5.2 0.1 copy.27
  5.3 0.0 copy-done.2
  5.3 0.0 copy-start.3
  5.3 0.1 fusion
  5.4 0.3 copy.20
  5.7 0.1 copy.21
  5.8 0.3 copy.24
  6.1 0.1 copy.25
  6.2 0.1 add_bitcast_fusion
  6.3 0.1 copy-done.3
  6.4 0.0 copy-start
  6.4 0.0 copy-start.1
  6.4 0.4 copy_bitcast_fusion
  6.8 0.4 copy-done
  7.2 0.0 copy-done.1
  7.2 53.4 %shard_map.118 = (f32[2,16,384]{2,1,0:T(8,128)S(1)}, f32[9,64,64]{2,1,0:T(8,128)S(1)}, f32[9,2,64]{2,1,0:T(2,128)S(1)}, f32[24,128]{1,0:T(8,128)S(1)}) custom-call(f32[2,16,384]{2,1,0:T(8,128)S(1)} %copy-done, bf16[2,16,384]{2,1,0:T(8,128)(2,1)S(1)} %copy-done.1, bf16[16,64,384]{2,1,0:T(8,128)(2,1)S(1)} %get-tuple-element.23.pre1, ...), custom_call_target="tpu_custom_call" | custom-call | tf_op jit(solution)/shard_map/pallas_call | solution.py:362
  60.6 0.6 slice_bitcast_fusion
  61.2 0.6 reshape.51
  61.8 0.6 copy.36
  62.4 0.7 %copy.37 = f32[9,64,64]{2,1,0:T(8,128)} copy(f32[9,64,64]{2,1,0:T(8,128)S(1)} %get-tuple-element.32) | data formatting | bytes 294912
  63.1 0.6 copy.38
  (5 shorter events, 0.1 us)
Async XLA Ops:
  1.3 0.7 %copy-start.4 = (bf16[9,2,64]{2,1,0:T(2,128)(2,1)S(1)}, bf16[9,2,64]{2,1,0:T(2,128)(2,1)}, u32[]{:S(2)}) copy-start(bf16[9,2,64]{2,1,0:T(2,128)(2,1)} %param.13) | copy-start | bytes 6916
  3.2 2.0 %copy-start.2 = (bf16[64,16,384]{2,1,0:T(8,128)(2,1)S(1)}, bf16[64,16,384]{2,1,0:T(8,128)(2,1)}, u32[]{:S(2)}) copy-start(bf16[64,16,384]{2,1,0:T(8,128)(2,1)} %param.10) | copy-start | bytes 2359300
  5.3 1.1 %copy-start.3 = (bf16[64,16,384]{2,1,0:T(8,128)(2,1)S(1)}, bf16[64,16,384]{2,1,0:T(8,128)(2,1)}, u32[]{:S(2)}) copy-start(bf16[64,16,384]{2,1,0:T(8,128)(2,1)} %param.9) | copy-start | bytes 2359300
  6.4 0.8 %copy-start = (f32[2,16,384]{2,1,0:T(8,128)S(1)}, f32[2,16,384]{2,1,0:T(8,128)}, u32[]{:S(2)}) copy-start(f32[2,16,384]{2,1,0:T(8,128)} %cot.1) | copy-start | bytes 147460
  6.4 0.8 %copy-start.1 = (bf16[2,16,384]{2,1,0:T(8,128)(2,1)S(1)}, bf16[2,16,384]{2,1,0:T(8,128)(2,1)}, u32[]{:S(2)}) copy-start(bf16[2,16,384]{2,1,0:T(8,128)(2,1)} %vel.1) | copy-start | bytes 73732

commit v3 on v2

--- a/solution.py
+++ b/solution.py
@@ -59,7 +59,7 @@
     nx, ny, factor, cot, vel, pre1, pre2, edges, w_last, w_middle, w_first,
     spread_out, middle_out, last_out, small_out,
     cot_pad, vel_pad, edge_in, halo1, halo2, slots_y, slots_x, grads, sums_x, sums_y, gathered, few_y, few_x,
-    adj, adj_rolled, vel_rolled, slope1, slope2, hidden1, hidden2, stack, taps, spread, gm, gl, gf,
+    adj, adj_rolled, vel_rolled, slope1, slope2, hidden1, hidden2, acc, taps, spread, gm, gl, gf,
     send, recv, send_y, recv_y, send_x, recv_x,
 ):
     rows, cols = cot.shape[1], cot.shape[2]
@@ -105,14 +105,18 @@
     gm[...] = jnp.zeros_like(gm)
     gl[...] = jnp.zeros_like(gl)
     gf[...] = jnp.zeros_like(gf)
-    taps[...] = jnp.zeros_like(taps)
+    tap = lax.broadcasted_iota(jnp.int32, taps.shape, 1)
+    taps[...] = jnp.where(tap == 18, 1.0, 0.0)
+    hidden1[0:3] = jnp.zeros((3, ch, cols), bf16)
+    hidden1[rows + 3 : rows + 6] = jnp.zeros((3, ch, cols), bf16)
+    acc[0:2] = jnp.zeros((2,) + acc.shape[1:], f32)
 
     def activate(r, _):
         value, slope = gelu_both(pre2[r].astype(f32))
         hidden2[r] = value.astype(bf16)
         slope2[r + 2, :, 0:cols] = slope
         value, slope = gelu_both(pre1[r].astype(f32))
-        hidden1[r] = value.astype(bf16)
+        hidden1[r + 3] = value.astype(bf16)
         slope1[r + 1, :, 0:cols] = slope
         return 0
 
@@ -240,33 +244,43 @@
                 taps[which, 2 * t + k : 2 * t + k + 1, :] = source[2 * (b + 1) + k, pl.ds(row + sign * a, 1), :]
 
     def first(i, own):
-        gather(0, adj_rolled, rows + i - 2, -1)
-        shifted = taps[0].astype(bf16)
-        delta = (dot(w_last[...], shifted, NN) * slope2[i]).astype(bf16)
-        wide = delta.astype(f32)
-        base = pl.multiple_of(i * (3 * ch), 3 * ch)
-        stack[pl.ds(base, ch), :] = roll_to(wide, -1, 1).astype(bf16)
-        stack[pl.ds(base + ch, ch), :] = delta
-        stack[pl.ds(base + 2 * ch, ch), :] = roll_to(wide, 1, 1).astype(bf16)
+        pair = (i, i + 1)
+        for at_pair, row in enumerate(pair):
+            gather(at_pair, adj_rolled, rows + row - 2, -1)
+        shifted = [taps[at_pair].astype(bf16) for at_pair in range(2)]
+        deltas = [(dot(w_last[...], x, NN) * slope2[row]).astype(bf16) for x, row in zip(shifted, pair)]
+        stacks = []
+        for delta in deltas:
+            wide = delta.astype(f32)
+            stacks.append(
+                jnp.concatenate(
+                    [roll_to(wide, -1, 1).astype(bf16), delta, roll_to(wide, 1, 1).astype(bf16)], axis=0
+                )
+            )
+        products = [dot(w_middle[...], x, NN) for x in stacks]
+        rights = [hidden1[pl.ds(row, 3)].reshape(3 * ch, cols) for row in pair]
+        gm[...] += dot(stacks[0][:, 0:cols], rights[0], NT) + dot(stacks[1][:, 0:cols], rights[1], NT)
         if own:
-            gl[...] += dot(shifted[:, 0:cols], hidden2[i - 2], NT)
+            both = [jnp.concatenate([hidden2[row - 2], d[:, 0:cols]], axis=0) for row, d in zip(pair, deltas)]
+            gl[...] += dot(shifted[0][:, 0:cols], both[0], NT) + dot(shifted[1][:, 0:cols], both[1], NT)
+        y, z = products
+        acc[i] += y[0:ch]
+        acc[i + 1] += y[ch : 2 * ch] + z[0:ch]
+        acc[i + 2] = y[2 * ch : 3 * ch] + z[ch : 2 * ch]
+        acc[i + 3] = z[2 * ch : 3 * ch]
         return 0
 
-    for low, high, own in ((0, 2, False), (2, rows + 2, True), (rows + 2, rows + 4, False)):
-        lax.fori_loop(low, high, lambda i, _, own=own: first(i, own), 0)
-
-    def middle(r, _):
-        base = pl.multiple_of((r + 1) * (3 * ch), 3 * ch)
-        gm[...] += dot(stack[pl.ds(base, 9 * ch), 0:cols], hidden1[r], NT)
-        return 0
-
-    lax.fori_loop(0, rows, middle, 0)
+    first(0, False)
+    lax.fori_loop(0, rows // 2, lambda k, _: first(2 * k + 2, True), 0)
+    first(rows + 2, False)
     half = 9 * ch // 2
     chunk = grads.shape[1]
     total_rows = nx * chunk
-    lower = jnp.concatenate([gl[0:24], jnp.zeros((24, ch), f32)], axis=1)
-    packed = jnp.concatenate([gm[0:half], gm[half : 2 * half]], axis=1)
-    packed = jnp.concatenate([packed, lower, jnp.zeros((total_rows - half - 24, 128), f32)], axis=0)
+    third = 3 * ch // 2
+    packed = jnp.concatenate([gm[0:third, 128:192], gm[third : 2 * third, 128:192]], axis=1)
+    packed = jnp.concatenate(
+        [gm[:, 0:128], packed, gl[0:24], jnp.zeros((total_rows - half - 24, 128), f32)], axis=0
+    )
     for k in range(nx):
         grads[k] = packed[k * chunk : (k + 1) * chunk]
     scatter = [
@@ -280,39 +294,35 @@
         copy.start()
     sums_x[gx] = grads[gx]
 
-    ones_row = lax.broadcasted_iota(jnp.int32, (32, cols), 0) == 18
-
-    def second(j, own):
-        base = pl.multiple_of(j * (3 * ch), 3 * ch)
-        delta = dot(w_middle[...], stack[pl.ds(base, 9 * ch), :], NN) * slope1[j]
-        delta = delta.astype(bf16)
-        e = dot(w_first[...], delta, NN)
-        f = roll_to(e[0:8], -1, 1) + e[8:16] + roll_to(e[16:24], 1, 1)
-        f = f[:, 0:cols]
-        for a in (-1, 0, 1):
-            for k in range(2):
-                row = 2 * (a + 1) + k
-                spread[k, pl.ds(j + 1 + a, 1), :] += f[row : row + 1, :]
+    def second(pair, own):
+        deltas = [(acc[j + 2] * slope1[j]).astype(bf16) for j in pair]
+        products = [dot(w_first[...], x, NN) for x in deltas]
         if own:
-            gather(1, vel_rolled, rows + j - 1, 1)
-            taken = jnp.where(ones_row, 1.0, taps[1][:, 0:cols]).astype(bf16)
-            delta2 = stack[pl.ds(base + 4 * ch, ch), 0:cols]
-            gf[...] += dot(taken, jnp.concatenate([delta[:, 0:cols], delta2], axis=0), NT)
+            for at_pair, j in enumerate(pair):
+                gather(2 + at_pair, vel_rolled, rows + j - 1, 1)
+            taken = [taps[2 + at_pair][:, 0:cols].astype(bf16) for at_pair in range(2)]
+            gf[...] += dot(taken[0], deltas[0][:, 0:cols], NT) + dot(taken[1], deltas[1][:, 0:cols], NT)
+        for j, e in zip(pair, products):
+            f = roll_to(e[0:8], -1, 1) + e[8:16] + roll_to(e[16:24], 1, 1)
+            f = f[:, 0:cols]
+            for a in (-1, 0, 1):
+                for k in range(2):
+                    row = 2 * (a + 1) + k
+                    spread[k, pl.ds(j + 1 + a, 1), :] += f[row : row + 1, :]
         return 0
 
-    half_way = rows // 2 + 1
-    second(0, False)
-    lax.fori_loop(1, half_way, lambda j, _: second(j, True), 0)
+    quarter = rows // 4
+    second((0, rows + 1), False)
+    lax.fori_loop(0, quarter, lambda k, _: second((2 * k + 1, 2 * k + 2), True), 0)
     sums_y[gy] = finish(sums_x, nx, scatter)
     started = begin(sums_y, gy, along_y, sems_y, 1)
-    lax.fori_loop(half_way, rows + 1, lambda j, _: second(j, True), 0)
-    few_y[gy] = gf[0:24]
+    lax.fori_loop(quarter, rows // 2, lambda k, _: second((2 * k + 1, 2 * k + 2), True), 0)
+    few_y[gy] = jnp.concatenate([gf[0:24], jnp.zeros((24, ch), f32)], axis=1)
     few = begin(few_y, gy, along_y, sems_y, 2)
     gathered[gx] = factor * finish(sums_y, ny, started)
     spreading = begin(gathered, gx, along_x, sems_x, 2)
     few_x[gx] = finish(few_y, ny, few)
     few = begin(few_x, gx, along_x, sems_x, 3)
-    second(rows + 1, False)
     for k in range(2):
         spread_out[k] = adj[k, rows : 2 * rows, 0:cols] + spread[k, 2 : rows + 2, :]
     for copy in cot_copies + edge_copies + row_copies + vel_copies:
@@ -322,17 +332,19 @@
     for copy in spreading:
         copy.wait_send()
     whole = jnp.concatenate([gathered[k] for k in range(nx)], axis=0)
-    for place_at in range(9):
-        t = 3 * (2 - place_at // 3) + place_at % 3
-        start = place_at * ch
+    for t in range(9):
+        a, start = t // 3, (t % 3) * ch
         for low in range(0, ch, 32):
             here = start + low
-            side = 0 if here < half else 64
-            here = here % half
+            side = a * ch
+            if a == 2:
+                side = 0 if here < third else 64
+                here = 3 * ch + here % third
             middle_out[t, low : low + 32, :] = whole[here : here + 32, side : side + ch]
     for t in range(9):
         last_out[t] = whole[half + 2 * t : half + 2 * t + 2, 0:ch]
-    small_out[...] = factor * finish(few_x, nx, few)
+    small_out[0] = factor * finish(few_x, nx, few)
+    small_out[1] = whole[half : half + 24]
 
 
 def per_device(nx, ny, cotangent, velocity_in, hidden_pre1, hidden_pre2, w_first, w_middle, w_last):
@@ -352,7 +364,7 @@
 
     edges = jnp.stack([edge(0), edge(cols - 2)])
     w_l = jnp.pad(w_last.reshape(18, ch), ((0, 14), (0, 0))).T
-    w_m = w_middle.reshape(3, 3, ch, ch)[::-1].reshape(9 * ch, ch).T
+    w_m = w_middle.reshape(3, 3, ch, ch).transpose(0, 3, 1, 2).reshape(3 * ch, 3 * ch)
     w_f = w_first.reshape(3, 3, ch, 2).transpose(1, 0, 3, 2).reshape(3, 6, ch)
     w_f = jnp.pad(w_f, ((0, 0), (0, 2), (0, 0))).reshape(24, ch)
     packed = 9 * ch // 2 + 24
@@ -365,7 +377,7 @@
             jax.ShapeDtypeStruct((2, rows, cols), f32),
             jax.ShapeDtypeStruct((9, ch, ch), f32),
             jax.ShapeDtypeStruct((9, 2, ch), f32),
-            jax.ShapeDtypeStruct((24, 128), f32),
+            jax.ShapeDtypeStruct((2, 24, 128), f32),
         ),
         in_specs=[vmem] * 8,
         out_specs=(vmem,) * 4,
@@ -388,14 +400,14 @@
             pltpu.VMEM((6, 3 * rows, wide), f32),
             pltpu.VMEM((rows + 2, ch, wide), f32),
             pltpu.VMEM((rows + 4, ch, wide), f32),
+            pltpu.VMEM((rows + 6, ch, cols), bf16),
             pltpu.VMEM((rows, ch, cols), bf16),
-            pltpu.VMEM((rows, ch, cols), bf16),
-            pltpu.VMEM(((rows + 4) * 3 * ch, wide), bf16),
-            pltpu.VMEM((2, 32, wide), f32),
+            pltpu.VMEM((rows + 6, ch, wide), f32),
+            pltpu.VMEM((4, 32, wide), f32),
             pltpu.VMEM((2, rows + 8, cols), f32),
-            pltpu.VMEM((9 * ch, ch), f32),
+            pltpu.VMEM((3 * ch, 3 * ch), f32),
+            pltpu.VMEM((32, 2 * ch), f32),
             pltpu.VMEM((32, ch), f32),
-            pltpu.VMEM((32, 2 * ch), f32),
             dma((4, 8)), dma((4, 8)),
             dma((3, ny)), dma((3, ny)), dma((4, nx)), dma((4, nx)),
         ],
@@ -403,8 +415,8 @@
             collective_id=0, has_side_effects=True, vmem_limit_bytes=48 * 2**20
         ),
     )(cotangent, velocity_in, pre1, pre2, edges, w_l, w_m, w_f)
-    grad_first = small[:18, :ch].reshape(9, 2, ch).transpose(0, 2, 1)
-    return grad_velocity, grad_first, grad_middle, grad_last, small[18, :ch], small[18, ch:]
+    grad_first = small[0, :18, :ch].reshape(9, 2, ch).transpose(0, 2, 1)
+    return grad_velocity, grad_first, grad_middle, grad_last, small[0, 18, :ch], small[1, 18, ch:]
 
 
 def solution(mesh):

time: 64 us -> 60.7 us (0.948)
  Pallas kernels: 53.4 us -> 49.9 us
    pallas_call x1, Pallas kernels: 53.4 us -> 49.9 us  [per_device(): pl.pallas_call(functools.partial(fused_kernel, nx, ny, factor), out_shape...]
    rev x1 -> x0, local copies, waits for them, and re-layouts: 0.92 us -> none  [per_device(): w_m = w_middle.reshape(3, 3, ch, ch)[::-1].reshape(9 * ch, ch).T]
where the time goes in v3:
time: 60.7 us; the launch traced here: 60.4 us
  Pallas kernels  49.9 us (82%)
  local copies, waits for them, and re-layouts  9.69 us (16%)
  between operations  0.73 us (1%)
    pallas_call x1, Pallas kernels, per_device(): pl.pallas_call(functools.partial(fused_kernel, nx, ny, factor), out_shape...  49.9 us
    unnamed x13, local copies, waits for them, and re-layouts  3.12 us
    slice x3, local copies, waits for them, and re-layouts, edge(): first = hidden_pre1[:, :, low:low + 2].reshape(ch, 2 * rows).astype(f32)  1.81 us
    reshape x2, local copies, waits for them, and re-layouts, per_device(): w_middle.reshape(3, 3, ch, ch).transpose(0, 3, 1, 2).reshape(3 * ch, 3 * ch)  1.23 us

profile of v3, /device:TPU:0, one launch (start us, length us, event | category | flops | bytes accessed | tf_op | source)
XLA Modules:
  0.0 60.4 jit_solution(16401652531240406995)
XLA Ops:
  0.6 0.7 %copy.30 = bf16[3,3,2,64]{3,2,1,0:T(2,128)(2,1)S(1)} copy(bf16[3,3,2,64]{3,2,0,1:T(2,128)(2,1)} %bitcast.33) | data formatting | bytes 4608 | tf_op jit(solution)/shard_map/transpose | solution.py:368
  1.3 0.0 copy-start.4
  1.4 0.7 %copy-done.4 = bf16[9,2,64]{2,1,0:T(2,128)(2,1)S(1)} copy-done((bf16[9,2,64]{2,1,0:T(2,128)(2,1)S(1)}, bf16[9,2,64]{2,1,0:T(2,128)(2,1)}, u32[]{:S(2)}) %copy-start.4) | copy-done | bytes 2328
  2.1 0.1 copy.28
  2.2 1.1 %copy.29 = bf16[3,3,64,64]{2,1,3,0:T(4,128)(2,1)S(1)} copy(bf16[3,3,64,64]{3,2,1,0:T(8,128)(2,1)} %bitcast.27) | data formatting | bytes 147456 | tf_op jit(solution)/shard_map/reshape | solution.py:367
  3.3 0.2 reshape.44.w_middle
  3.4 0.0 copy-start.2
  3.4 1.2 %fusion.1 = (bf16[64,16,2]{2,1,0:T(8,128)(2,1)S(1)}, bf16[64,16,2]{2,1,0:T(8,128)(2,1)S(1)}) fusion(bf16[64,16,384]{2,1,0:T(8,128)(2,1)} %param.9), kind=kLoop, calls=%fused_computation.10 | loop fusion | bytes 16384 | tf_op jit(solution)/shard_map/slice | solution.py:361
  4.7 0.3 copy.22
  4.9 0.1 copy.23
  5.0 0.3 copy.26
  5.3 0.1 copy.27
  5.4 0.0 copy-done.2
  5.4 0.0 copy-start.3
  5.5 0.1 fusion
  5.6 0.3 copy.20
  5.9 0.1 copy.21
  6.0 0.3 copy.24
  6.3 0.1 copy.25
  6.4 0.1 add_bitcast_fusion
  6.5 0.1 copy-done.3
  6.6 0.0 copy-start
  6.6 0.0 copy-start.1
  6.6 0.4 copy_bitcast_fusion
  7.0 0.4 copy-done
  7.4 0.0 copy-done.1
  7.4 49.9 %shard_map.118 = (f32[2,16,384]{2,1,0:T(8,128)S(1)}, f32[9,64,64]{2,1,0:T(8,128)S(1)}, f32[9,2,64]{2,1,0:T(2,128)S(1)}, f32[2,24,128]{2,1,0:T(8,128)S(1)}) custom-call(f32[2,16,384]{2,1,0:T(8,128)S(1)} %copy-done, bf16[2,16,384]{2,1,0:T(8,128)(2,1)S(1)} %copy-done.1, bf16[16,64,384]{2,1,0:T(8,128)(2,1)S(1)} %get-tuple-element.23.pre1, ...), custom_call_target="tpu_custom_call" | custom-call | tf_op jit(solution)/shard_map/pallas_call | solution.py:374
  57.3 0.6 slice_bitcast_fusion
  57.9 0.6 %reshape_squeeze.3 = f32[9,2,64]{2,1,0:T(2,128)} reshape(f32[1,18,64]{2,1,0:T(8,128)S(1)} %slice.25) | data formatting | bytes 9216 | tf_op jit(solution)/shard_map/reshape;squeeze | solution.py:418
  58.5 0.6 %copy.36 = f32[2,16,384]{2,1,0:T(8,128)} copy(f32[2,16,384]{2,1,0:T(8,128)S(1)} %get-tuple-element.30) | data formatting | bytes 98304
  59.1 0.7 %copy.37 = f32[9,64,64]{2,1,0:T(8,128)} copy(f32[9,64,64]{2,1,0:T(8,128)S(1)} %get-tuple-element.32) | data formatting | bytes 294912
  59.8 0.6 copy.38
  (6 shorter events, 0.1 us)
Async XLA Ops:
  1.3 0.7 %copy-start.4 = (bf16[9,2,64]{2,1,0:T(2,128)(2,1)S(1)}, bf16[9,2,64]{2,1,0:T(2,128)(2,1)}, u32[]{:S(2)}) copy-start(bf16[9,2,64]{2,1,0:T(2,128)(2,1)} %param.13) | copy-start | bytes 6916
  3.4 2.0 %copy-start.2 = (bf16[64,16,384]{2,1,0:T(8,128)(2,1)S(1)}, bf16[64,16,384]{2,1,0:T(8,128)(2,1)}, u32[]{:S(2)}) copy-start(bf16[64,16,384]{2,1,0:T(8,128)(2,1)} %param.10) | copy-start | bytes 2359300
  5.4 1.1 %copy-start.3 = (bf16[64,16,384]{2,1,0:T(8,128)(2,1)S(1)}, bf16[64,16,384]{2,1,0:T(8,128)(2,1)}, u32[]{:S(2)}) copy-start(bf16[64,16,384]{2,1,0:T(8,128)(2,1)} %param.9) | copy-start | bytes 2359300
  6.6 0.8 %copy-start = (f32[2,16,384]{2,1,0:T(8,128)S(1)}, f32[2,16,384]{2,1,0:T(8,128)}, u32[]{:S(2)}) copy-start(f32[2,16,384]{2,1,0:T(8,128)} %cot.1) | copy-start | bytes 147460
  6.6 0.8 %copy-start.1 = (bf16[2,16,384]{2,1,0:T(8,128)(2,1)S(1)}, bf16[2,16,384]{2,1,0:T(8,128)(2,1)}, u32[]{:S(2)}) copy-start(bf16[2,16,384]{2,1,0:T(8,128)(2,1)} %vel.1) | copy-start | bytes 73732

commit v4 on v3

--- a/solution.py
+++ b/solution.py
@@ -56,10 +56,10 @@
 
 
 def fused_kernel(
-    nx, ny, factor, cot, vel, pre1, pre2, edges, w_last, w_middle, w_first,
+    nx, ny, factor, cot, vel, pre1, pre2, w_last, w_taps, w_first,
     spread_out, middle_out, last_out, small_out,
     cot_pad, vel_pad, edge_in, halo1, halo2, slots_y, slots_x, grads, sums_x, sums_y, gathered, few_y, few_x,
-    adj, adj_rolled, vel_rolled, slope1, slope2, hidden1, hidden2, acc, taps, spread, gm, gl, gf,
+    adj, adj_rolled, vel_rolled, slope1, slope2, hidden1, hidden2, acc, edges, w_middle, taps, spread, gm, gl, gf,
     send, recv, send_y, recv_y, send_x, recv_x,
 ):
     rows, cols = cot.shape[1], cot.shape[2]
@@ -97,8 +97,22 @@
         remote(pre1.at[rows - 1 : rows], halo1.at[0:1], 3, 2, at(1, 0)),
         remote(pre1.at[0:1], halo1.at[1:2], 3, 3, at(-1, 0)),
     ]
-    for copy in cot_copies + edge_copies + row_copies + vel_copies:
+    for copy in cot_copies + row_copies:
         copy.start()
+    lane = lax.broadcasted_iota(jnp.int32, (ch, 128), 1)
+    for side in range(2):
+        low = (cols - 128) * side
+        built = jnp.zeros((ch, 128), f32)
+        for r in range(rows):
+            for source, to_lane in ((pre2, 2 * r + 4), (pre1, 2 * r + 66)):
+                moved = roll_to(source[r, :, low : low + 128].astype(f32), to_lane - 126 * side, 1)
+                built = jnp.where((lane == to_lane) | (lane == to_lane + 1), moved, built)
+        edges[side] = built.astype(bf16)
+    for copy in edge_copies + vel_copies:
+        copy.start()
+    turned = [w_taps[3 * a : 3 * a + 3].astype(f32).reshape(3 * ch, ch) for a in range(3)]
+    for a in range(3):
+        w_middle[a * ch : (a + 1) * ch, :] = turned[a].T.astype(bf16)
     cot_pad[:, rows : 2 * rows, 0:cols] = cot[...]
     vel_pad[:, rows : 2 * rows, 0:cols] = vel[...]
     spread[...] = jnp.zeros_like(spread)
@@ -171,14 +185,14 @@
 
     for copy in row_copies + edge_copies:
         copy.wait_recv()
-    lane = lax.broadcasted_iota(jnp.int32, (ch, 128), 1)
     place = lax.rem(lane, 64)
     top = place < jnp.where(lane < 64, 4, 2)
     bottom = place >= jnp.where(lane < 64, 36, 34)
     sides = []
     for side in range(2):
-        mid = jnp.where(top, pltpu.roll(edge_in[side, 0], 96, 1), edge_in[side, 1])
-        sides.append(jnp.where(bottom, pltpu.roll(edge_in[side, 2], 32, 1), mid))
+        above, beside, below = (edge_in[side, k].astype(f32) for k in range(3))
+        mid = jnp.where(top, pltpu.roll(above, 96, 1), beside)
+        sides.append(jnp.where(bottom, pltpu.roll(below, 32, 1), mid))
 
     def edge_slope(offset):
         right = pltpu.roll(sides[0], lax.rem(256 - offset, 128), 1)
@@ -357,14 +371,7 @@
     pre1 = jnp.transpose(hidden_pre1, (1, 0, 2))
     pre2 = jnp.transpose(hidden_pre2, (1, 0, 2))
 
-    def edge(low):
-        first = hidden_pre1[:, :, low : low + 2].reshape(ch, 2 * rows).astype(f32)
-        second = hidden_pre2[:, :, low : low + 2].reshape(ch, 2 * rows).astype(f32)
-        return jnp.pad(second, ((0, 0), (4, 124 - 2 * rows))) + jnp.pad(first, ((0, 0), (66, 62 - 2 * rows)))
-
-    edges = jnp.stack([edge(0), edge(cols - 2)])
     w_l = jnp.pad(w_last.reshape(18, ch), ((0, 14), (0, 0))).T
-    w_m = w_middle.reshape(3, 3, ch, ch).transpose(0, 3, 1, 2).reshape(3 * ch, 3 * ch)
     w_f = w_first.reshape(3, 3, ch, 2).transpose(1, 0, 3, 2).reshape(3, 6, ch)
     w_f = jnp.pad(w_f, ((0, 0), (0, 2), (0, 0))).reshape(24, ch)
     packed = 9 * ch // 2 + 24
@@ -379,12 +386,12 @@
             jax.ShapeDtypeStruct((9, 2, ch), f32),
             jax.ShapeDtypeStruct((2, 24, 128), f32),
         ),
-        in_specs=[vmem] * 8,
+        in_specs=[vmem] * 7,
         out_specs=(vmem,) * 4,
         scratch_shapes=[
             pltpu.VMEM((2, 3 * rows, cols + 256), f32),
             pltpu.VMEM((2, 3 * rows, cols + 256), bf16),
-            pltpu.VMEM((2, 3, ch, 128), f32),
+            pltpu.VMEM((2, 3, ch, 128), bf16),
             pltpu.VMEM((2, ch, cols), bf16),
             pltpu.VMEM((4, ch, cols), bf16),
             pltpu.VMEM((ny, 8, 128), f32),
@@ -403,6 +410,8 @@
             pltpu.VMEM((rows + 6, ch, cols), bf16),
             pltpu.VMEM((rows, ch, cols), bf16),
             pltpu.VMEM((rows + 6, ch, wide), f32),
+            pltpu.VMEM((2, ch, 128), bf16),
+            pltpu.VMEM((3 * ch, 3 * ch), bf16),
             pltpu.VMEM((4, 32, wide), f32),
             pltpu.VMEM((2, rows + 8, cols), f32),
             pltpu.VMEM((3 * ch, 3 * ch), f32),
@@ -414,7 +423,7 @@
         compiler_params=pltpu.CompilerParams(
             collective_id=0, has_side_effects=True, vmem_limit_bytes=48 * 2**20
         ),
-    )(cotangent, velocity_in, pre1, pre2, edges, w_l, w_m, w_f)
+    )(cotangent, velocity_in, pre1, pre2, w_l, w_middle, w_f)
     grad_first = small[0, :18, :ch].reshape(9, 2, ch).transpose(0, 2, 1)
     return grad_velocity, grad_first, grad_middle, grad_last, small[0, 18, :ch], small[1, 18, ch:]
 

time: 60.7 us -> 56.3 us (0.928)
  local copies, waits for them, and re-layouts: 9.69 us -> 6.47 us
  Pallas kernels: 49.9 us -> 48.9 us
    slice x6 -> x0, local copies, waits for them, and re-layouts: 2.51 us -> none  [the longest x3 1.81 us: edge(): first = hidden_pre1[:, :, low:low + 2].reshape(ch, 2 * rows).astype(f32)]
    transpose x1, local copies, waits for them, and re-layouts: 0.38 us -> 1.8 us  [per_device(): pre2 = jnp.transpose(hidden_pre2, (1, 0, 2))]
    reshape x2 -> x0, local copies, waits for them, and re-layouts: 1.23 us -> none  [per_device(): w_middle.reshape(3, 3, ch, ch).transpose(0, 3, 1, 2).reshape(3 * ch, 3 * ch)]
    pallas_call x1, Pallas kernels: 49.9 us -> 48.9 us  [per_device(): pl.pallas_call(functools.partial(fused_kernel, nx, ny, factor), out_shape...]
    unnamed x13 -> x11, local copies, waits for them, and re-layouts: 3.12 us -> 2.61 us
where the time goes in v4:
time: 56.3 us; the launch traced here: 56.1 us
  Pallas kernels  48.9 us (87%)
  local copies, waits for them, and re-layouts  6.47 us (11%)
  between operations  0.71 us (1%)
    pallas_call x1, Pallas kernels, per_device(): pl.pallas_call(functools.partial(fused_kernel, nx, ny, factor), out_shape...  48.9 us
    unnamed x11, local copies, waits for them, and re-layouts  2.61 us
    transpose x1, local copies, waits for them, and re-layouts, per_device(): pre2 = jnp.transpose(hidden_pre2, (1, 0, 2))  1.8 us

profile of v4, /device:TPU:0, one launch (start us, length us, event | category | flops | bytes accessed | tf_op | source)
XLA Modules:
  0.0 56.1 jit_solution(13567245424815965275)
XLA Ops:
  0.6 0.7 %copy.20 = bf16[3,3,2,64]{3,2,1,0:T(2,128)(2,1)S(1)} copy(bf16[3,3,2,64]{3,2,0,1:T(2,128)(2,1)} %bitcast.17) | data formatting | bytes 4608 | tf_op jit(solution)/shard_map/transpose | solution.py:375
  1.3 0.0 copy-start.3
  1.4 0.7 %copy-done.3 = bf16[9,2,64]{2,1,0:T(2,128)(2,1)S(1)} copy-done((bf16[9,2,64]{2,1,0:T(2,128)(2,1)S(1)}, bf16[9,2,64]{2,1,0:T(2,128)(2,1)}, u32[]{:S(2)}) %copy-start.3) | copy-done | bytes 2328
  2.1 0.1 copy.19
  2.2 0.0 copy-start
  2.2 0.0 copy-start.1
  2.2 0.0 copy-start.2
  2.2 1.8 %copy_bitcast_fusion = (bf16[16,64,384]{2,1,0:T(8,128)(2,1)S(1)}, bf16[16,64,384]{2,1,0:T(8,128)(2,1)S(1)}) fusion(bf16[64,16,384]{2,1,0:T(8,128)(2,1)} %param.10, bf16[64,16,384]{2,1,0:T(8,128)(2,1)} %param.9), kind=kLoop, calls=%fused_computation | loop fusion | bytes 3145728 | tf_op jit(solution)/shard_map/transpose | solution.py:372
  4.0 0.0 copy-done
  4.0 0.0 copy-done.1
  4.0 0.0 copy-done.2
  4.0 48.9 %shard_map.118 = (f32[2,16,384]{2,1,0:T(8,128)S(1)}, f32[9,64,64]{2,1,0:T(8,128)S(1)}, f32[9,2,64]{2,1,0:T(2,128)S(1)}, f32[2,24,128]{2,1,0:T(8,128)S(1)}) custom-call(f32[2,16,384]{2,1,0:T(8,128)S(1)} %copy-done.1, bf16[2,16,384]{2,1,0:T(8,128)(2,1)S(1)} %copy-done.2, bf16[16,64,384]{2,1,0:T(8,128)(2,1)S(1)} %get-tuple-element.17.pre1, ...), custom_call_target="tpu_custom_call" | custom-call | tf_op jit(solution)/shard_map/pallas_call | solution.py:381
  52.9 0.6 %slice_bitcast_fusion = (f32[64]{0:T(128)}, f32[64]{0:T(128)}) fusion(f32[2,24,128]{2,1,0:T(8,128)S(1)} %get-tuple-element.11), kind=kLoop, calls=%fused_computation.4 | loop fusion | bytes 1024 | tf_op jit(solution)/shard_map/squeeze | solution.py:428
  53.5 0.6 %reshape_squeeze.3 = f32[9,2,64]{2,1,0:T(2,128)} reshape(f32[1,18,64]{2,1,0:T(8,128)S(1)} %slice.9) | data formatting | bytes 9216 | tf_op jit(solution)/shard_map/reshape;squeeze | solution.py:427
  54.1 0.6 %copy.26 = f32[2,16,384]{2,1,0:T(8,128)} copy(f32[2,16,384]{2,1,0:T(8,128)S(1)} %get-tuple-element.24) | data formatting | bytes 98304
  54.8 0.7 %copy.27 = f32[9,64,64]{2,1,0:T(8,128)} copy(f32[9,64,64]{2,1,0:T(8,128)S(1)} %get-tuple-element.26) | data formatting | bytes 294912
  55.5 0.6 %copy.28 = f32[9,2,64]{2,1,0:T(2,128)} copy(f32[9,2,64]{2,1,0:T(2,128)S(1)} %get-tuple-element.27) | data formatting | bytes 9216
  (5 shorter events, 0.1 us)
Async XLA Ops:
  1.3 0.7 %copy-start.3 = (bf16[9,2,64]{2,1,0:T(2,128)(2,1)S(1)}, bf16[9,2,64]{2,1,0:T(2,128)(2,1)}, u32[]{:S(2)}) copy-start(bf16[9,2,64]{2,1,0:T(2,128)(2,1)} %param.13) | copy-start | bytes 6916
  2.2 1.8 %copy-start = (bf16[9,64,64]{2,1,0:T(8,128)(2,1)S(1)}, bf16[9,64,64]{2,1,0:T(8,128)(2,1)}, u32[]{:S(2)}) copy-start(bf16[9,64,64]{2,1,0:T(8,128)(2,1)} %w_taps.1) | copy-start | bytes 221188
  2.2 1.8 %copy-start.1 = (f32[2,16,384]{2,1,0:T(8,128)S(1)}, f32[2,16,384]{2,1,0:T(8,128)}, u32[]{:S(2)}) copy-start(f32[2,16,384]{2,1,0:T(8,128)} %cot.1) | copy-start | bytes 147460
  2.2 1.8 %copy-start.2 = (bf16[2,16,384]{2,1,0:T(8,128)(2,1)S(1)}, bf16[2,16,384]{2,1,0:T(8,128)(2,1)}, u32[]{:S(2)}) copy-start(bf16[2,16,384]{2,1,0:T(8,128)(2,1)} %vel.1) | copy-start | bytes 73732
